TPU v7x, 128 devices: a whole 4x4x4 slice. The times are simulated.
128 devices in a mesh: seq: 16 (over x, z), dp: 8 (over y, core).
Axes of the slice: x: 4, y: 4, z: 4, core: 2. Of those that a mesh axis runs over, the one named last changes fastest.
Arguments:
- layer_input: bfloat16 [8, 2048, 4096], P('dp', 'seq'), may hold values from -6 to 6
- query_rows: bfloat16 [8, 2048, 4096], P('dp', 'seq')
- key_rows: bfloat16 [8, 2048, 4096], P('dp', 'seq')
- value_rows: bfloat16 [8, 2048, 4096], P('dp', 'seq'), may hold values from -6 to 6
- out_grad: bfloat16 [8, 2048, 4096], P('dp', 'seq'), may hold values from -6 to 6
- neighbours: int32 [8, 16, 8], P('dp'), may hold values from 0 to 15, as said below
- counts: int32 [8, 16], P('dp'), may hold values from 1 to 8, as said below
Outputs:
- query_grad: bfloat16 [8, 2048, 4096], P('dp', 'seq')
- key_grad: bfloat16 [8, 2048, 4096], P('dp', 'seq')
- value_grad: bfloat16 [8, 2048, 4096], P('dp', 'seq')
- weight_grad: float32 [3, 4096, 4096], P(None, 'dp', 'seq')
Inputs may be any that keep to these rules, and one draw needn't show every extreme that they name: `neighbours`: each row lists 8 distinct key blocks of the same snapshot, the query block itself first; entries past counts are not attended. `counts`: every snapshot has a query block with 8.
All inputs are finite; a program needn't handle non-finite values.
Results may differ from a plain program's by a relative error of at most 0.015.
Values may be sent and summed in bfloat16 or wider, within the bound.
A program may use at most 192 MiB of HBM per device.

v0:
```python
import math

import jax
import jax.numpy as jnp
from jax import lax
from jax.sharding import PartitionSpec as P

HDIM = 128
BLK = 128
MAXNB = 8


def block_backward(query_cols, key_cols, value_cols, grad_cols, links, tallies):
    score_scale = HDIM ** (-0.5)
    rows_total = query_cols.shape[0]
    width_cols = query_cols.shape[1]
    heads_cols = width_cols // HDIM
    block_count = rows_total // BLK
    query_blocks = query_cols.reshape(block_count, BLK, heads_cols, HDIM)
    key_near = key_cols.reshape(block_count, BLK, heads_cols, HDIM)[links].reshape(
        block_count, MAXNB * BLK, heads_cols, HDIM
    )
    value_near = value_cols.reshape(block_count, BLK, heads_cols, HDIM)[links].reshape(
        block_count, MAXNB * BLK, heads_cols, HDIM
    )
    grad_blocks = grad_cols.reshape(block_count, BLK, heads_cols, HDIM)
    live_slot = jnp.arange(MAXNB)[None, :] < tallies[:, None]
    live_keys = jnp.repeat(live_slot, BLK, axis=1)[:, None, None, :]
    scores = (
        jnp.einsum("nthd,nkhd->nhtk", query_blocks, key_near, preferred_element_type=jnp.float32)
        * score_scale
    )
    scores = jnp.where(live_keys, scores, -jnp.inf)
    top_score = jnp.max(scores, axis=-1, keepdims=True)
    weights = jnp.exp(scores - top_score)
    probs = weights / jnp.sum(weights, axis=-1, keepdims=True)
    probs_low = probs.astype(jnp.bfloat16)
    value_part = jnp.einsum(
        "nhtk,nthd->nkhd", probs_low, grad_blocks, preferred_element_type=jnp.float32
    )
    prob_grad = jnp.einsum(
        "nthd,nkhd->nhtk", grad_blocks, value_near, preferred_element_type=jnp.float32
    )
    row_dot = jnp.sum(probs * prob_grad, axis=-1, keepdims=True)
    score_grad = (probs * (prob_grad - row_dot) * score_scale).astype(jnp.bfloat16)
    query_part = jnp.einsum(
        "nhtk,nkhd->nthd", score_grad, key_near, preferred_element_type=jnp.float32
    )
    key_part = jnp.einsum(
        "nhtk,nthd->nkhd", score_grad, query_blocks, preferred_element_type=jnp.float32
    )
    flat_links = links.reshape(-1)
    key_sum = (
        jnp.zeros((block_count, BLK, heads_cols, HDIM), jnp.float32)
        .at[flat_links]
        .add(key_part.reshape(block_count * MAXNB, BLK, heads_cols, HDIM))
    )
    value_sum = (
        jnp.zeros((block_count, BLK, heads_cols, HDIM), jnp.float32)
        .at[flat_links]
        .add(value_part.reshape(block_count * MAXNB, BLK, heads_cols, HDIM))
    )
    return (
        query_part.reshape(rows_total, width_cols).astype(jnp.bfloat16),
        key_sum.reshape(rows_total, width_cols).astype(jnp.bfloat16),
        value_sum.reshape(rows_total, width_cols).astype(jnp.bfloat16),
    )


def local(layer_input, query_rows, key_rows, value_rows, out_grad, neighbours, counts):
    seq_count = lax.axis_size("seq")
    dp_count = lax.axis_size("dp")
    width_here = query_rows.shape[2] // seq_count
    query_here, key_here, value_here, grad_here = (
        lax.all_to_all(query_rows, "seq", split_axis=2, concat_axis=1, tiled=True),
        lax.all_to_all(key_rows, "seq", split_axis=2, concat_axis=1, tiled=True),
        lax.all_to_all(value_rows, "seq", split_axis=2, concat_axis=1, tiled=True),
        lax.all_to_all(out_grad, "seq", split_axis=2, concat_axis=1, tiled=True),
    )
    snap_tokens = query_here.shape[1]
    heads_here = width_here // HDIM
    query_flat = query_here[0]
    key_flat = key_here[0]
    value_flat = value_here[0]
    grad_flat = grad_here[0]
    links = neighbours[0]
    tallies = counts[0]
    empty = jnp.zeros((snap_tokens, width_here), jnp.bfloat16)

    def head_step(head_index, carried):
        first_col = head_index * HDIM
        pieces = [
            lax.dynamic_slice_in_dim(array, first_col, HDIM, 1)
            for array in (query_flat, key_flat, value_flat, grad_flat)
        ]
        outputs = block_backward(pieces[0], pieces[1], pieces[2], pieces[3], links, tallies)
        return tuple(
            (
                lax.dynamic_update_slice_in_dim(carried[i], outputs[i], first_col, 1)
                for i in range(3)
            )
        )

    query_back, key_back, value_back = lax.fori_loop(
        0, heads_here, head_step, (empty, empty, empty)
    )
    query_grad, key_grad, value_grad = (
        lax.all_to_all(query_back[None], "seq", split_axis=1, concat_axis=2, tiled=True),
        lax.all_to_all(key_back[None], "seq", split_axis=1, concat_axis=2, tiled=True),
        lax.all_to_all(value_back[None], "seq", split_axis=1, concat_axis=2, tiled=True),
    )
    norm_factor = 1.0 / math.sqrt(snap_tokens * dp_count)
    shard_piece = lax.all_gather(layer_input, "seq", axis=1, tiled=True)
    terms = [
        jnp.dot(shard_piece[0].T, grad_part, preferred_element_type=jnp.float32)
        for grad_part in (query_back, key_back, value_back)
    ]
    summed = jnp.stack(terms, axis=0)
    owned = lax.psum_scatter(
        summed.astype(jnp.bfloat16), "dp", scatter_dimension=1, tiled=True
    ).astype(jnp.float32)
    return (query_grad, key_grad, value_grad, owned * norm_factor)


def solution(mesh):
    placed = (
        P("dp", "seq", None),
        P("dp", "seq", None),
        P("dp", "seq", None),
        P("dp", "seq", None),
        P("dp", "seq", None),
        P("dp", None, None),
        P("dp", None),
    )
    return jax.shard_map(
        local,
        mesh=mesh,
        in_specs=placed,
        out_specs=(
            P("dp", "seq", None),
            P("dp", "seq", None),
            P("dp", "seq", None),
            P(None, "dp", "seq"),
        ),
        check_vma=False,
    )
```

profile of v0, /device:TPU:18, one launch (start us, length us, event | category | flops | bytes accessed | tf_op | source)
XLA Modules:
  0.0 599.5 jit_solution(623852219905623241)
XLA Ops:
  7.9 5.0 copy.74
  13.5 22.3 %reduce.12 = bf16[4096,128]{1,0:T(8,128)(2,1)S(1)} reduce(bf16[4096,1,128]{2,1,0:T(2,128)(2,1)S(1)} %bitcast.230, bf16[]{:T(256)} %broadcast.125), dimensions={1}, to_apply=%bitcast.96.reduce_sub_computation | reduce | bytes 2097154
  36.9 8.3 %all-to-all-start = ((bf16[16,2,16384]{2,1,0:T(2,128)(2,1)}), bf16[16,2,16384]{2,1,0:T(2,128)(2,1)S(1)}, u32[]{:S(2)}, u32[]{:S(2)}) async-start(bf16[16,2,16384]{2,1,0:T(2,128)(2,1)} %reshape.260), calls=%async_computation | async-start | bytes 2097152 | tf_op jit(solution)/shard_map/all_to_all | solution.py:76
  45.2 5.0 copy.76
  50.3 23.3 %reduce.13 = bf16[4096,128]{1,0:T(8,128)(2,1)} reduce(bf16[4096,1,128]{2,1,0:T(2,128)(2,1)S(1)} %bitcast.234, bf16[]{:T(256)} %broadcast.125), dimensions={1}, to_apply=%bitcast.98.reduce_sub_computation | reduce | bytes 2097154
  73.5 2.2 reshape.262
  75.7 7.8 %all-to-all-start.1 = ((bf16[16,2,16384]{2,1,0:T(2,128)(2,1)}), bf16[16,2,16384]{2,1,0:T(2,128)(2,1)}, u32[]{:S(2)}, u32[]{:S(2)}) async-start(bf16[16,2,16384]{2,1,0:T(2,128)(2,1)} %reshape.262), calls=%async_computation.1 | async-start | bytes 2097152 | tf_op jit(solution)/shard_map/all_to_all | solution.py:75
  83.5 5.1 copy.78
  88.6 23.3 %reduce.14 = bf16[4096,128]{1,0:T(8,128)(2,1)} reduce(bf16[4096,1,128]{2,1,0:T(2,128)(2,1)S(1)} %bitcast.235, bf16[]{:T(256)} %broadcast.125), dimensions={1}, to_apply=%bitcast.100.reduce_sub_computation | reduce | bytes 2097154
  111.9 2.2 reshape.264
  114.1 7.2 %all-to-all-start.2 = ((bf16[16,2,16384]{2,1,0:T(2,128)(2,1)}), bf16[16,2,16384]{2,1,0:T(2,128)(2,1)}, u32[]{:S(2)}, u32[]{:S(2)}) async-start(bf16[16,2,16384]{2,1,0:T(2,128)(2,1)} %reshape.264), calls=%async_computation.2 | async-start | bytes 2097152 | tf_op jit(solution)/shard_map/all_to_all | solution.py:78
  121.3 5.0 copy.80
  126.3 23.3 %reduce.15 = bf16[4096,128]{1,0:T(8,128)(2,1)} reduce(bf16[4096,1,128]{2,1,0:T(2,128)(2,1)S(1)} %bitcast.236, bf16[]{:T(256)} %broadcast.125), dimensions={1}, to_apply=%bitcast.102.reduce_sub_computation | reduce | bytes 2097154
  149.6 2.1 reshape.266
  151.7 7.2 %all-to-all-start.3 = ((bf16[16,2,16384]{2,1,0:T(2,128)(2,1)}), bf16[16,2,16384]{2,1,0:T(2,128)(2,1)}, u32[]{:S(2)}, u32[]{:S(2)}) async-start(bf16[16,2,16384]{2,1,0:T(2,128)(2,1)} %reshape.266), calls=%async_computation.3 | async-start | bytes 2097152 | tf_op jit(solution)/shard_map/all_to_all | solution.py:77
  161.9 1.5 copy.75
  163.4 4.3 reshape.263
  168.9 2.3 copy.77
  171.1 4.3 reshape.265
  176.6 2.3 copy.79
  178.8 4.3 reshape.267
  184.3 2.3 copy.81
  189.6 259.0 %while.18 = (s32[]{:T(128)}, bf16[2048,256]{1,0:T(8,128)(2,1)}, bf16[2048,256]{1,0:T(8,128)(2,1)}, bf16[2048,256]{1,0:T(8,128)(2,1)}, bf16[2048,256]{1,0:T(8,128...) while((s32[]{:T(128)}, bf16[2048,256]{1,0:T(8,128)(2,1)}, ...), condition=%wide.wide.region_6.7_spmd, body=%wide.wide.region_0.6_spmd.sunk | while | flops 2731287552 | bytes 208251984 | solution.py:104
  190.0 3.1 gather_fusion
  195.3 3.1 gather_fusion.1
  198.4 6.8 %fusion.115 = f32[16,128,1024]{2,1,0:T(8,128)} fusion(bf16[16,128,128]{2,1,0:T(8,128)(2,1)S(1)} %bitcast.213, bf16[16,1024,128]{2,1,0:T(8,128)(2,1)} %bitcast.208), kind=kOutput, calls=%fused_computation.61.clone.clone.1 | convolution fusion | flops 536870912 | bytes 13107200 | tf_op jit(solution)/shard_map/while/body/eval_jaxpr/nthd,nkhd->nhtk/dot_general | solution.py:41
  205.4 8.1 %fusion.116 = (f32[16,128]{1,0:T(8,128)S(1)}, f32[16,128,1024]{2,1,0:T(8,128)}) fusion(pred[16,1024]{1,0:T(8,128)(4,1)S(1)} %bitcast.248, bf16[16,128,128]{2,1,0:T(8,128)(2,1)S(1)} %bitcast.215, bf16[16,1024,128]{2,1,0:T(8,128)(2,1)} %bitcast.209), kind=kOutput, calls=%fused_computation.57.clone.clone.1 | convolution fusion | flops 545260544 | bytes 13131776 | tf_op jit(solution)/shard_map/while/body/eval_jaxpr/sub | solution.py:35
  213.5 18.8 %fusion.117 = bf16[16,128,128]{1,2,0:T(8,128)(2,1)S(1)} fusion(bf16[16,1024,128]{2,1,0:T(8,128)(2,1)} %bitcast.210, f32[16,128,1024]{2,1,0:T(8,128)} %fusion.115, f32[16,128,1024]{2,1,0:T(8,128)} %get-tuple-element.419, f32[16,128]{1,0:T(8,128)S(1)} %get-tuple-element.420), kind=kOutput, calls=%fused_computation.22.clone.clone.1 | convolution fusion | flops 551816192 | bytes 21504000 | tf_op jit(solution)/shard_map/while/body/eval_jaxpr/nhtk,nkhd->nthd/dot_general | solution.py:46
  233.1 7.9 %fusion.119 = f32[16,1024,1,128]{1,3,0,2:T(8,128)} fusion(bf16[16,128,128]{2,1,0:T(8,128)(2,1)S(1)} %bitcast.214, f32[16,128,1024]{2,1,0:T(8,128)} %get-tuple-element.419, f32[16,128]{1,0:T(8,128)S(1)} %get-tuple-element.420), kind=kOutput, calls=%fused_computation.21.clone.clone.1 | convolution fusion | flops 541065216 | bytes 17309696 | tf_op jit(solution)/shard_map/while/body/eval_jaxpr/nhtk,nthd->nkhd/dot_general | solution.py:38
  241.0 9.2 %copy.121 = f32[16,1024,1,128]{3,1,0,2:T(8,128)} copy(f32[16,1024,1,128]{1,3,0,2:T(8,128)} %fusion.119) | data formatting | bytes 16777216 | tf_op jit(solution)/shard_map/while/body/eval_jaxpr/nhtk,nthd->nkhd/transpose | solution.py:38
  250.3 17.0 %scatter_fusion = f32[16,128,128]{2,1,0:T(8,128)S(1)} fusion(f32[16,128,128]{2,1,0:T(8,128)S(1)} %broadcast.161.clone, s32[128]{0:T(128)S(1)} %fusion.118, f32[128,128,128]{2,1,0:T(8,128)} %bitcast.207), kind=kCustom, calls=%fused_computation.3.clone.clone.1 | custom fusion | flops 2097152 | bytes 25166336 | tf_op jit(solution)/shard_map/while/body/eval_jaxpr/scatter-add | solution.py:61
  267.5 24.1 %fusion.120 = f32[16,1024,1,128]{1,3,0,2:T(8,128)} fusion(bf16[16,128,128]{2,1,0:T(8,128)(2,1)S(1)} %bitcast.216, f32[16,128,1024]{2,1,0:T(8,128)} %fusion.115, f32[16,128,1024]{2,1,0:T(8,128)} %get-tuple-element.419, f32[16,128]{1,0:T(8,128)S(1)} %get-tuple-element.420), kind=kOutput, calls=%fused_computation.20.clone.clone.1 | convolution fusion | flops 551554048 | bytes 25698304 | tf_op jit(solution)/shard_map/while/body/eval_jaxpr/nhtk,nthd->nkhd/dot_general | solution.py:49
  291.6 9.3 %copy.122 = f32[16,1024,1,128]{3,1,0,2:T(8,128)} copy(f32[16,1024,1,128]{1,3,0,2:T(8,128)} %fusion.120) | data formatting | bytes 16777216 | tf_op jit(solution)/shard_map/while/body/eval_jaxpr/nhtk,nthd->nkhd/transpose | solution.py:49
  300.9 17.0 %scatter_fusion.1 = f32[16,128,128]{2,1,0:T(8,128)S(1)} fusion(f32[16,128,128]{2,1,0:T(8,128)S(1)} %broadcast.161.clone.1, s32[128]{0:T(128)S(1)} %fusion.118, f32[128,128,128]{2,1,0:T(8,128)} %bitcast.206), kind=kCustom, calls=%fused_computation.2.clone.clone.1 | custom fusion | flops 2097152 | bytes 25166336 | tf_op jit(solution)/shard_map/while/body/eval_jaxpr/scatter-add | solution.py:56
  319.4 3.1 gather_fusion
  324.6 3.1 gather_fusion.1
  327.7 6.8 %fusion.115 = f32[16,128,1024]{2,1,0:T(8,128)} fusion(bf16[16,128,128]{2,1,0:T(8,128)(2,1)S(1)} %bitcast.213, bf16[16,1024,128]{2,1,0:T(8,128)(2,1)} %bitcast.208), kind=kOutput, calls=%fused_computation.61.clone.clone.1 | convolution fusion | flops 536870912 | bytes 13107200 | tf_op jit(solution)/shard_map/while/body/eval_jaxpr/nthd,nkhd->nhtk/dot_general | solution.py:41
  334.7 8.1 %fusion.116 = (f32[16,128]{1,0:T(8,128)S(1)}, f32[16,128,1024]{2,1,0:T(8,128)}) fusion(pred[16,1024]{1,0:T(8,128)(4,1)S(1)} %bitcast.248, bf16[16,128,128]{2,1,0:T(8,128)(2,1)S(1)} %bitcast.215, bf16[16,1024,128]{2,1,0:T(8,128)(2,1)} %bitcast.209), kind=kOutput, calls=%fused_computation.57.clone.clone.1 | convolution fusion | flops 545260544 | bytes 13131776 | tf_op jit(solution)/shard_map/while/body/eval_jaxpr/sub | solution.py:35
  342.8 18.8 %fusion.117 = bf16[16,128,128]{1,2,0:T(8,128)(2,1)S(1)} fusion(bf16[16,1024,128]{2,1,0:T(8,128)(2,1)} %bitcast.210, f32[16,128,1024]{2,1,0:T(8,128)} %fusion.115, f32[16,128,1024]{2,1,0:T(8,128)} %get-tuple-element.419, f32[16,128]{1,0:T(8,128)S(1)} %get-tuple-element.420), kind=kOutput, calls=%fused_computation.22.clone.clone.1 | convolution fusion | flops 551816192 | bytes 21504000 | tf_op jit(solution)/shard_map/while/body/eval_jaxpr/nhtk,nkhd->nthd/dot_general | solution.py:46
  362.4 7.9 %fusion.119 = f32[16,1024,1,128]{1,3,0,2:T(8,128)} fusion(bf16[16,128,128]{2,1,0:T(8,128)(2,1)S(1)} %bitcast.214, f32[16,128,1024]{2,1,0:T(8,128)} %get-tuple-element.419, f32[16,128]{1,0:T(8,128)S(1)} %get-tuple-element.420), kind=kOutput, calls=%fused_computation.21.clone.clone.1 | convolution fusion | flops 541065216 | bytes 17309696 | tf_op jit(solution)/shard_map/while/body/eval_jaxpr/nhtk,nthd->nkhd/dot_general | solution.py:38
  370.3 9.2 %copy.121 = f32[16,1024,1,128]{3,1,0,2:T(8,128)} copy(f32[16,1024,1,128]{1,3,0,2:T(8,128)} %fusion.119) | data formatting | bytes 16777216 | tf_op jit(solution)/shard_map/while/body/eval_jaxpr/nhtk,nthd->nkhd/transpose | solution.py:38
  379.6 17.0 %scatter_fusion = f32[16,128,128]{2,1,0:T(8,128)S(1)} fusion(f32[16,128,128]{2,1,0:T(8,128)S(1)} %broadcast.161.clone, s32[128]{0:T(128)S(1)} %fusion.118, f32[128,128,128]{2,1,0:T(8,128)} %bitcast.207), kind=kCustom, calls=%fused_computation.3.clone.clone.1 | custom fusion | flops 2097152 | bytes 25166336 | tf_op jit(solution)/shard_map/while/body/eval_jaxpr/scatter-add | solution.py:61
  396.8 24.1 %fusion.120 = f32[16,1024,1,128]{1,3,0,2:T(8,128)} fusion(bf16[16,128,128]{2,1,0:T(8,128)(2,1)S(1)} %bitcast.216, f32[16,128,1024]{2,1,0:T(8,128)} %fusion.115, f32[16,128,1024]{2,1,0:T(8,128)} %get-tuple-element.419, f32[16,128]{1,0:T(8,128)S(1)} %get-tuple-element.420), kind=kOutput, calls=%fused_computation.20.clone.clone.1 | convolution fusion | flops 551554048 | bytes 25698304 | tf_op jit(solution)/shard_map/while/body/eval_jaxpr/nhtk,nthd->nkhd/dot_general | solution.py:49
  420.9 9.3 %copy.122 = f32[16,1024,1,128]{3,1,0,2:T(8,128)} copy(f32[16,1024,1,128]{1,3,0,2:T(8,128)} %fusion.120) | data formatting | bytes 16777216 | tf_op jit(solution)/shard_map/while/body/eval_jaxpr/nhtk,nthd->nkhd/transpose | solution.py:49
  430.3 17.0 %scatter_fusion.1 = f32[16,128,128]{2,1,0:T(8,128)S(1)} fusion(f32[16,128,128]{2,1,0:T(8,128)S(1)} %broadcast.161.clone.1, s32[128]{0:T(128)S(1)} %fusion.118, f32[128,128,128]{2,1,0:T(8,128)} %bitcast.206), kind=kCustom, calls=%fused_computation.2.clone.clone.1 | custom fusion | flops 2097152 | bytes 25166336 | tf_op jit(solution)/shard_map/while/body/eval_jaxpr/scatter-add | solution.py:56
  448.7 10.8 %fusion.50 = bf16[1,4096,256]{1,2,0:T(8,128)(2,1)S(1)} fusion(bf16[2048,256]{1,0:T(8,128)(2,1)} %get-tuple-element.192, bf16[1,2048,4096]{2,1,0:T(8,128)(2,1)} %all-gather.2.cloned.1.call-done), kind=kOutput, calls=%fused_computation.53 | convolution fusion | flops 4296015872 | bytes 19922944 | tf_op jit(solution)/shard_map/dot_general | solution.py:115
  459.7 4.7 fusion.53
  464.5 4.7 fusion.56
  469.2 3.1 pad_maximum_fusion
  472.4 12.9 %copy.110 = bf16[1,2048,256]{2,0,1:T(2,128)(2,1)} copy(bf16[1,2048,256]{2,1,0:T(8,128)(2,1)S(1)} %bitcast.220) | data formatting | bytes 2097152 | tf_op jit(solution)/shard_map/broadcast_in_dim | solution.py:108
  485.3 12.1 %reduce.16 = bf16[2048,256]{1,0:T(8,128)(2,1)S(1)} reduce(bf16[2048,1,256]{2,1,0:T(2,128)(2,1)} %bitcast.232, bf16[]{:T(256)} %broadcast.125), dimensions={1}, to_apply=%bitcast.128.reduce_sub_computation | reduce | bytes 2097154
  498.5 7.2 %all-to-all-start.4 = ((bf16[16,2,16384]{2,1,0:T(2,128)(2,1)}), bf16[16,2,16384]{2,1,0:T(2,128)(2,1)S(1)}, u32[]{:S(2)}, u32[]{:S(2)}) async-start(bf16[16,2,16384]{2,1,0:T(2,128)(2,1)} %reshape.268), calls=%async_computation.4 | async-start | bytes 2097152 | tf_op jit(solution)/shard_map/all_to_all | solution.py:108
  505.7 12.9 %copy.109 = bf16[1,2048,256]{2,0,1:T(2,128)(2,1)} copy(bf16[1,2048,256]{2,1,0:T(8,128)(2,1)S(1)} %bitcast.221) | data formatting | bytes 2097152 | tf_op jit(solution)/shard_map/broadcast_in_dim | solution.py:109
  518.7 11.6 %reduce.17 = bf16[2048,256]{1,0:T(8,128)(2,1)S(1)} reduce(bf16[2048,1,256]{2,1,0:T(2,128)(2,1)} %bitcast.233, bf16[]{:T(256)} %broadcast.125), dimensions={1}, to_apply=%bitcast.127.reduce_sub_computation | reduce | bytes 2097154
  531.3 7.5 %all-to-all-start.5 = ((bf16[16,2,16384]{2,1,0:T(2,128)(2,1)}), bf16[16,2,16384]{2,1,0:T(2,128)(2,1)}, u32[]{:S(2)}, u32[]{:S(2)}) async-start(bf16[16,2,16384]{2,1,0:T(2,128)(2,1)} %reshape.270), calls=%async_computation.5 | async-start | bytes 2097152 | tf_op jit(solution)/shard_map/all_to_all | solution.py:109
  538.9 11.7 %copy.108 = bf16[1,2048,256]{2,0,1:T(2,128)(2,1)S(1)} copy(bf16[1,2048,256]{2,1,0:T(8,128)(2,1)S(1)} %bitcast.222) | data formatting | bytes 2097152 | tf_op jit(solution)/shard_map/broadcast_in_dim | solution.py:110
  550.7 10.5 %reduce.18 = bf16[2048,256]{1,0:T(8,128)(2,1)S(1)} reduce(bf16[2048,1,256]{2,1,0:T(2,128)(2,1)S(1)} %bitcast.231, bf16[]{:T(256)} %broadcast.125), dimensions={1}, to_apply=%bitcast.126.reduce_sub_computation | reduce | bytes 2097154
  562.3 7.2 %all-to-all-start.6 = ((bf16[16,2,16384]{2,1,0:T(2,128)(2,1)}), bf16[16,2,16384]{2,1,0:T(2,128)(2,1)S(1)}, u32[]{:S(2)}, u32[]{:S(2)}) async-start(bf16[16,2,16384]{2,1,0:T(2,128)(2,1)} %reshape.272), calls=%async_computation.6 | async-start | bytes 2097152 | tf_op jit(solution)/shard_map/all_to_all | solution.py:110
  569.5 4.3 reshape.269
  575.0 1.6 copy.84
  577.9 4.3 reshape.271
  583.4 1.6 copy.86
  589.5 1.3 convert_multiply_fusion
  590.9 1.6 copy.92
  (92 shorter events, 33.1 us)
Async XLA Ops:
  7.2 441.5 %all-gather.2.cloned.1.call-start = ((), (), s32[]{:S(2)}) async-start(), calls=%async_computation.8 | async-start | bytes 17825792 | tf_op jit(solution)/shard_map/all_gather | solution.py:113
  36.9 38.8 %all-to-all-start = ((bf16[16,2,16384]{2,1,0:T(2,128)(2,1)}), bf16[16,2,16384]{2,1,0:T(2,128)(2,1)S(1)}, u32[]{:S(2)}, u32[]{:S(2)}) async-start(bf16[16,2,16384]{2,1,0:T(2,128)(2,1)} %reshape.260), calls=%async_computation | async-start | bytes 2097152 | tf_op jit(solution)/shard_map/all_to_all | solution.py:76
  75.7 38.4 %all-to-all-start.1 = ((bf16[16,2,16384]{2,1,0:T(2,128)(2,1)}), bf16[16,2,16384]{2,1,0:T(2,128)(2,1)}, u32[]{:S(2)}, u32[]{:S(2)}) async-start(bf16[16,2,16384]{2,1,0:T(2,128)(2,1)} %reshape.262), calls=%async_computation.1 | async-start | bytes 2097152 | tf_op jit(solution)/shard_map/all_to_all | solution.py:75
  88.6 70.4 %copy-start.6 = (s32[1,16,8]{1,2,0:T(8,128)S(1)}, s32[1,16,8]{1,2,0:T(8,128)}, u32[]{:S(2)}) copy-start(s32[1,16,8]{1,2,0:T(8,128)} %param.14) | copy-start | bytes 1540
  114.1 37.7 %all-to-all-start.2 = ((bf16[16,2,16384]{2,1,0:T(2,128)(2,1)}), bf16[16,2,16384]{2,1,0:T(2,128)(2,1)}, u32[]{:S(2)}, u32[]{:S(2)}) async-start(bf16[16,2,16384]{2,1,0:T(2,128)(2,1)} %reshape.264), calls=%async_computation.2 | async-start | bytes 2097152 | tf_op jit(solution)/shard_map/all_to_all | solution.py:78
  151.7 27.1 %all-to-all-start.3 = ((bf16[16,2,16384]{2,1,0:T(2,128)(2,1)}), bf16[16,2,16384]{2,1,0:T(2,128)(2,1)}, u32[]{:S(2)}, u32[]{:S(2)}) async-start(bf16[16,2,16384]{2,1,0:T(2,128)(2,1)} %reshape.266), calls=%async_computation.3 | async-start | bytes 2097152 | tf_op jit(solution)/shard_map/all_to_all | solution.py:77
  159.0 430.6 %reduce-scatter.2.cloned.1.call-start = ((), (), s32[]{:S(2)}) async-start(), calls=%async_computation.9 | async-start | bytes 7077888 | tf_op jit(solution)/shard_map/reduce_scatter | solution.py:119
  159.1 0.6 copy-start.7
  175.4 14.2 %copy-start.8 = (s32[1,16]{1,0:T(1,128)S(1)}, s32[1,16]{1,0:T(1,128)}, u32[]{:S(2)}) copy-start(s32[1,16]{1,0:T(1,128)} %param.15) | copy-start | bytes 196
  198.4 6.9 %copy-start.1 = (bf16[2048,256]{1,0:T(8,128)(2,1)S(1)}, bf16[2048,256]{1,0:T(8,128)(2,1)}, u32[]{:S(2)}) copy-start(bf16[2048,256]{1,0:T(8,128)(2,1)} %get-tuple-element.464) | copy-start | bytes 3145732 | tf_op jit(solution)/shard_map/while
  327.7 6.9 %copy-start.1 = (bf16[2048,256]{1,0:T(8,128)(2,1)S(1)}, bf16[2048,256]{1,0:T(8,128)(2,1)}, u32[]{:S(2)}) copy-start(bf16[2048,256]{1,0:T(8,128)(2,1)} %get-tuple-element.464) | copy-start | bytes 3145732 | tf_op jit(solution)/shard_map/while
  448.7 10.9 %copy-start = (bf16[1,2048,4096]{2,1,0:T(8,128)(2,1)S(1)}, bf16[1,2048,4096]{2,1,0:T(8,128)(2,1)}, u32[]{:S(2)}) copy-start(bf16[1,2048,4096]{2,1,0:T(8,128)(2,1)} %all-gather.2.cloned.1.call-done) | copy-start | bytes 50331652
  448.7 11.1 %copy-start.3 = (bf16[2048,256]{1,0:T(8,128)(2,1)S(1)}, bf16[2048,256]{1,0:T(8,128)(2,1)}, u32[]{:S(2)}) copy-start(bf16[2048,256]{1,0:T(8,128)(2,1)} %get-tuple-element.191) | copy-start | bytes 3145732
  459.7 4.7 copy-start.2
  485.3 53.6 %copy-start.4 = (bf16[2048,256]{1,0:T(8,128)(2,1)S(1)}, bf16[2048,256]{1,0:T(8,128)(2,1)}, u32[]{:S(2)}) copy-start(bf16[2048,256]{1,0:T(8,128)(2,1)} %get-tuple-element.192) | copy-start | bytes 3145732
  498.5 32.8 %all-to-all-start.4 = ((bf16[16,2,16384]{2,1,0:T(2,128)(2,1)}), bf16[16,2,16384]{2,1,0:T(2,128)(2,1)S(1)}, u32[]{:S(2)}, u32[]{:S(2)}) async-start(bf16[16,2,16384]{2,1,0:T(2,128)(2,1)} %reshape.268), calls=%async_computation.4 | async-start | bytes 2097152 | tf_op jit(solution)/shard_map/all_to_all | solution.py:108
  531.3 7.6 %copy-start.5 = (bf16[16,2,16384]{2,1,0:T(2,128)(2,1)}, bf16[16,2,16384]{2,1,0:T(2,128)(2,1)S(1)}, u32[]{:S(2)}) copy-start(bf16[16,2,16384]{2,1,0:T(2,128)(2,1)S(1)} %all-to-all-done.4) | copy-start | bytes 3145732
  531.3 31.0 %all-to-all-start.5 = ((bf16[16,2,16384]{2,1,0:T(2,128)(2,1)}), bf16[16,2,16384]{2,1,0:T(2,128)(2,1)}, u32[]{:S(2)}, u32[]{:S(2)}) async-start(bf16[16,2,16384]{2,1,0:T(2,128)(2,1)} %reshape.270), calls=%async_computation.5 | async-start | bytes 2097152 | tf_op jit(solution)/shard_map/all_to_all | solution.py:109
  562.3 24.0 %all-to-all-start.6 = ((bf16[16,2,16384]{2,1,0:T(2,128)(2,1)}), bf16[16,2,16384]{2,1,0:T(2,128)(2,1)S(1)}, u32[]{:S(2)}, u32[]{:S(2)}) async-start(bf16[16,2,16384]{2,1,0:T(2,128)(2,1)} %reshape.272), calls=%async_computation.6 | async-start | bytes 2097152 | tf_op jit(solution)/shard_map/all_to_all | solution.py:110
Sparse Core Ops, SparseCore 0:
  10.1 139.6 all-gather.1
  472.5 41.3 reduce-scatter.1
where the time goes:
time: 611 us; the launch traced here: 600 us
  other arithmetic  200 us (33%)
  local copies, waits for them, and re-layouts  180 us (29%)
  matrix products  151 us (25%)
  starting transfers between devices  52.6 us (9%)
  between operations  14.5 us (2%)
    unnamed x7, other arithmetic  126 us
    unnamed x46, local copies, waits for them, and re-layouts  68.5 us
    dot_general x2, matrix products, block_backward(): jnp.einsum('nhtk,nthd->nkhd', score_grad, query_blocks, preferred_element...  48.2 us
    dot_general x2, matrix products, block_backward(): jnp.einsum('nhtk,nkhd->nthd', score_grad, key_near, preferred_element_typ...  37.5 us
    scatter-add x2, other arithmetic, block_backward(): key_sum = jnp.zeros((block_count, BLK, heads_cols, HDIM), jnp.float32).at...  34.1 us
    scatter-add x2, other arithmetic, block_backward(): value_sum = jnp.zeros((block_count, BLK, heads_cols, HDIM), jnp.float32)....  34.1 us
    dot_general x3, matrix products, local(): jnp.dot(shard_piece[0].T, grad_part, preferred_element_type=jnp.float32)  20.3 us
    transpose x2, local copies, waits for them, and re-layouts, block_backward(): jnp.einsum('nhtk,nthd->nkhd', score_grad, query_blocks, preferred_element...  18.5 us
  transfers between devices with their start and end apart: 9, of which 0 were waited for; matrix products, arithmetic and copies ran while one was open for 84% of the time, Pallas kernels for 0%

commit v1 on v0

v1 whole, which is shorter than its diff:
```python
import functools
import math

import jax
import jax.numpy as jnp
from jax import lax
from jax.experimental import pallas as pl
from jax.experimental.pallas import tpu as pltpu
from jax.sharding import PartitionSpec as P

HDIM = 128
BLK = 128
MAXNB = 8
NQB = 16
SEQ = 16
SIDE = 4
COLS = 256
MESH = pl.DeviceIdType.MESH


def offsets():
    pairs = [(dx, dz) for dx in range(SIDE) for dz in range(SIDE) if dx or dz]
    far = lambda d: min(d, SIDE - d)
    return sorted(pairs, key=lambda p: -(far(p[0]) + far(p[1])))


def peer_of(me, dx, dz):
    x, z = me // SIDE, lax.rem(me, SIDE)
    return lax.rem(x + dx, SIDE) * SIDE + lax.rem(z + dz, SIDE)


def greet(me):
    barrier = pltpu.get_barrier_semaphore()
    for dx, dz in offsets():
        pl.semaphore_signal(
            barrier, inc=1, device_id={"seq": peer_of(me, dx, dz)}, device_id_type=MESH
        )
    pl.semaphore_wait(barrier, SEQ - 1)


def to_heads_kernel(count, *refs):
    ins, outs = refs[:count], refs[count : 2 * count]
    send_sem, recv_sem, own_sem = refs[2 * count :]
    me = lax.axis_index("seq")
    greet(me)
    rows = pl.ds(pl.multiple_of(me * BLK, BLK), BLK)
    copies = []
    for i, (dx, dz) in enumerate(offsets()):
        peer = peer_of(me, dx, dz)
        cols = pl.ds(pl.multiple_of(peer * COLS, COLS), COLS)
        for a in range(count):
            copy = pltpu.make_async_remote_copy(
                src_ref=ins[a].at[:, cols],
                dst_ref=outs[a].at[rows, :],
                send_sem=send_sem.at[a, i],
                recv_sem=recv_sem.at[a, i],
                device_id={"seq": peer},
                device_id_type=MESH,
            )
            copy.start()
            copies.append(copy)
    mine = pl.ds(pl.multiple_of(me * COLS, COLS), COLS)
    for a in range(count):
        own = pltpu.make_async_copy(ins[a].at[:, mine], outs[a].at[rows, :], own_sem.at[a])
        own.start()
        copies.append(own)
    for copy in copies:
        copy.wait()


def to_rows_kernel(count, *refs):
    ins, outs = refs[:count], refs[count : 2 * count]
    send_sem, recv_sem, own_sem = refs[2 * count :]
    me = lax.axis_index("seq")
    greet(me)
    mine = pl.ds(pl.multiple_of(me * COLS, COLS), COLS)
    copies = []
    for i, (dx, dz) in enumerate(offsets()):
        peer = peer_of(me, dx, dz)
        rows = pl.ds(pl.multiple_of(peer * BLK, BLK), BLK)
        for a in range(count):
            copy = pltpu.make_async_remote_copy(
                src_ref=ins[a].at[rows, :],
                dst_ref=outs[a].at[:, mine],
                send_sem=send_sem.at[a, i],
                recv_sem=recv_sem.at[a, i],
                device_id={"seq": peer},
                device_id_type=MESH,
            )
            copy.start()
            copies.append(copy)
    rows = pl.ds(pl.multiple_of(me * BLK, BLK), BLK)
    for a in range(count):
        own = pltpu.make_async_copy(ins[a].at[rows, :], outs[a].at[:, mine], own_sem.at[a])
        own.start()
        copies.append(own)
    for copy in copies:
        copy.wait()


def exchange(kernel, arrays, shape, collective_id):
    count = len(arrays)
    moved = count * SEQ * BLK * COLS * 2
    return pl.pallas_call(
        functools.partial(kernel, count),
        out_shape=[jax.ShapeDtypeStruct(shape, jnp.bfloat16)] * count,
        in_specs=[pl.BlockSpec(memory_space=pl.ANY)] * count,
        out_specs=[pl.BlockSpec(memory_space=pl.ANY)] * count,
        scratch_shapes=[
            pltpu.SemaphoreType.DMA((count, SEQ - 1)),
            pltpu.SemaphoreType.DMA((count, SEQ - 1)),
            pltpu.SemaphoreType.DMA((count,)),
        ],
        compiler_params=pltpu.CompilerParams(
            collective_id=collective_id, has_side_effects=True
        ),
        cost_estimate=pl.CostEstimate(flops=0, bytes_accessed=16 * moved, transcendentals=0),
    )(*arrays)


def attend(kv_links, tallies, q_ref, k_ref, v_ref, g_ref, dq_ref, dk_ref, dv_ref, wq, turned, acc, sp):
    scale = HDIM ** (-0.5)
    heads = COLS // HDIM
    f32 = jnp.float32
    acc[...] = jnp.zeros_like(acc)
    wq[...] = jnp.zeros_like(wq)

    @pl.loop(0, NQB)
    def _(n):
        rows = pl.ds(pl.multiple_of(n * BLK, BLK), BLK)
        for h in range(heads):
            turned[h, n] = k_ref[rows, h * HDIM : (h + 1) * HDIM].astype(f32).T.astype(jnp.bfloat16)

    @pl.loop(0, NQB)
    def _(b):
        mine = pl.ds(pl.multiple_of(b * BLK, BLK), BLK)
        tally = tallies[b]

        def variant(slots):
            for h in range(heads):
                cols = slice(h * HDIM, (h + 1) * HDIM)
                wq[h, :HDIM, :HDIM] = q_ref[mine, cols]
                wq[h, HDIM:, HDIM:] = g_ref[mine, cols]
            for h in range(heads):
                cols = slice(h * HDIM, (h + 1) * HDIM)
                both = wq[h]
                top = None
                for j in range(slots):
                    rows = pl.ds(pl.multiple_of(kv_links[b, j] * BLK, BLK), BLK)
                    kv = jnp.concatenate([k_ref[rows, cols], v_ref[rows, cols]], axis=1)
                    pair = lax.dot_general(
                        kv, both, (((1,), (1,)), ((), ())), preferred_element_type=f32
                    )
                    score = pair[:, :HDIM]
                    if j == slots - 1 and slots > 1:
                        score = jnp.where(j < tally, score, -jnp.inf)
                    sp[h, j, :, :HDIM] = score
                    sp[h, j, :, HDIM:] = pair[:, HDIM:]
                    here = jnp.max(score, axis=0, keepdims=True)
                    top = here if top is None else jnp.maximum(top, here)
                total = jnp.zeros((1, HDIM), f32)
                dot = jnp.zeros((1, HDIM), f32)
                for j in range(slots):
                    weight = jnp.exp((sp[h, j, :, :HDIM] - top) * scale)
                    sp[h, j, :, :HDIM] = weight
                    total += jnp.sum(weight, axis=0, keepdims=True)
                    dot += jnp.sum(weight * sp[h, j, :, HDIM:], axis=0, keepdims=True)
                inverse = 1.0 / total
                dot = dot * inverse
                dq = jnp.zeros((HDIM, BLK), f32)
                for j in range(slots):
                    link = kv_links[b, j]
                    rows = pl.ds(pl.multiple_of(link * BLK, BLK), BLK)
                    prob = sp[h, j, :, :HDIM] * inverse
                    slope = (prob * (sp[h, j, :, HDIM:] - dot) * scale).astype(jnp.bfloat16)
                    left = jnp.concatenate([slope, prob.astype(jnp.bfloat16)], axis=1)
                    acc[h, rows, :] += jnp.dot(left, both, preferred_element_type=f32)
                    dq += jnp.dot(turned[h, link], slope, preferred_element_type=f32)
                dq_ref[mine, cols] = dq.T.astype(jnp.bfloat16)

        for slots in range(2, MAXNB + 1, 2):
            pl.when((tally == slots) | (tally == slots - 1))(functools.partial(variant, slots))

    @pl.loop(0, NQB)
    def _(n):
        rows = pl.ds(pl.multiple_of(n * BLK, BLK), BLK)
        for h in range(heads):
            cols = slice(h * HDIM, (h + 1) * HDIM)
            dk_ref[rows, cols] = acc[h, rows, :HDIM].astype(jnp.bfloat16)
            dv_ref[rows, cols] = acc[h, rows, HDIM:].astype(jnp.bfloat16)


def attention(links, tallies, q, k, v, g):
    tokens = NQB * BLK
    heads = COLS // HDIM
    spec = pl.BlockSpec(memory_space=pltpu.VMEM)
    smem = pl.BlockSpec(memory_space=pltpu.SMEM)
    flops = heads * NQB * MAXNB * 5 * 2 * BLK**3
    return pl.pallas_call(
        attend,
        out_shape=[jax.ShapeDtypeStruct((tokens, COLS), jnp.bfloat16)] * 3,
        in_specs=[smem, smem] + [spec] * 4,
        out_specs=[spec] * 3,
        scratch_shapes=[
            pltpu.VMEM((heads, 2 * HDIM, 2 * BLK), jnp.bfloat16),
            pltpu.VMEM((heads, NQB, HDIM, BLK), jnp.bfloat16),
            pltpu.VMEM((heads, tokens, 2 * HDIM), jnp.float32),
            pltpu.VMEM((heads, MAXNB, BLK, 2 * BLK), jnp.float32),
        ],
        compiler_params=pltpu.CompilerParams(vmem_limit_bytes=40 << 20),
        cost_estimate=pl.CostEstimate(
            flops=flops, bytes_accessed=7 * tokens * COLS * 2, transcendentals=heads * NQB * MAXNB * BLK * BLK
        ),
    )(links, tallies, q, k, v, g)


def local(layer_input, query_rows, key_rows, value_rows, out_grad, neighbours, counts):
    dp_count = lax.axis_size("dp")
    tokens = NQB * BLK
    q, k, v, g = exchange(
        to_heads_kernel,
        [query_rows[0], key_rows[0], value_rows[0], out_grad[0]],
        (tokens, COLS),
        0,
    )
    whole = lax.all_gather(layer_input, "seq", axis=1, tiled=True)
    dq, dk, dv = attention(neighbours[0], counts[0], q, k, v, g)
    width = query_rows.shape[2]
    query_grad, key_grad, value_grad = exchange(
        to_rows_kernel, [dq, dk, dv], (BLK, width), 1
    )
    terms = [
        jnp.dot(whole[0].T, part, preferred_element_type=jnp.float32) for part in (dq, dk, dv)
    ]
    summed = jnp.stack(terms, axis=0).astype(jnp.bfloat16)
    owned = lax.psum_scatter(summed, "dp", scatter_dimension=1, tiled=True).astype(jnp.float32)
    norm_factor = 1.0 / math.sqrt(tokens * dp_count)
    return query_grad[None], key_grad[None], value_grad[None], owned * norm_factor


def solution(mesh):
    rows = P("dp", "seq", None)
    return jax.shard_map(
        local,
        mesh=mesh,
        in_specs=(rows,) * 5 + (P("dp", None, None), P("dp", None)),
        out_specs=(rows, rows, rows, P(None, "dp", "seq")),
        check_vma=False,
    )
```

time: 611 us -> 248 us (0.41)
  the two profiles are of different devices: /device:TPU:18 before, /device:TPU:1 now
where the time goes in v1:
time: 248 us; the launch traced here: 247 us
  Pallas kernels  152 us (61%)
  waiting for transfers between devices  43.3 us (17%)
  matrix products  19.8 us (8%)
  between operations  14.2 us (6%)
  local copies, waits for them, and re-layouts  13.3 us (5%)
  other arithmetic  4.47 us (2%)
    pallas_call x2, Pallas kernels, exchange(): pl.pallas_call(functools.partial(kernel, count), out_shape=[jax.ShapeDtyp...  125 us
    all_gather x1, waiting for transfers between devices, local(): whole = lax.all_gather(layer_input, 'seq', axis=1, tiled=True)  42.6 us
    pallas_call x1, Pallas kernels, attention(): pl.pallas_call(attend, out_shape=[jax.ShapeDtypeStruct((tokens, COLS), jn...  27 us
    dot_general x3, matrix products, local(): jnp.dot(whole[0].T, part, preferred_element_type=jnp.float32)  19.8 us
    unnamed x24, local copies, waits for them, and re-layouts  12.6 us
  transfers between devices with their start and end apart: 2, of which 1 were waited for; matrix products, arithmetic and copies ran while one was open for 0% of the time, Pallas kernels for 61%

profile of v1, /device:TPU:1, one launch (start us, length us, event | category | flops | bytes accessed | tf_op | source)
XLA Modules:
  0.0 246.8 jit_solution(9456295112523633681)
XLA Ops:
  7.2 0.0 copy-start.7
  7.2 0.0 all-gather.2.cloned.1.call-start
  7.2 0.7 all-gather.2.cloned.1.call-update
  7.9 0.0 reduce-scatter.2.cloned.1.call-start
  8.0 0.8 copy.11.kv_links
  8.7 78.5 %shard_map.102 = (bf16[2048,256]{1,0:T(8,128)(2,1)}, bf16[2048,256]{1,0:T(8,128)(2,1)}, bf16[2048,256]{1,0:T(8,128)(2,1)}, bf16[2048,256]{1,0:T(8,128)(2,1)}) custom-call(bf16[128,4096]{1,0:T(8,128)(2,1)} %bitcast.47, bf16[128,4096]{1,0:T(8,128)(2,1)} %bitcast.48, bf16[128,4096]{1,0:T(8,128)(2,1)} %bitcast.49, bf16[128,4096]{1,0:T(8,128)(2,1)} %bitcast.50), custom_call_target="tpu_custom_call" | custom-call | bytes 67108864 | tf_op jit(solution)/shard_map/pallas_call | solution.py:104
  87.2 0.0 copy-done.7
  87.2 0.0 copy-start.3
  87.2 1.2 copy-done.3
  88.4 0.0 copy-start.4
  88.4 1.2 copy-done.4
  89.6 0.0 copy-start.5
  89.6 1.2 copy-done.5
  90.9 0.0 copy-start.6
  90.9 1.5 copy-done.6
  92.4 27.0 %shard_map.103 = (bf16[2048,256]{1,0:T(8,128)(2,1)S(1)}, bf16[2048,256]{1,0:T(8,128)(2,1)S(1)}, bf16[2048,256]{1,0:T(8,128)(2,1)S(1)}) custom-call(s32[16,8]{1,0:T(8,128)S(1)} %copy.11.kv_links, s32[16]{0:T(128)S(1)} %bitcast.43, bf16[2048,256]{1,0:T(8,128)(2,1)S(1)} %copy-done.3, bf16[2048,256]{1,0:T(8,128)(2,1)S(1)} %copy-done.4, ...), custom_call_target="tpu_custom_call" | custom-call | flops 5368709120 | bytes 7340032 | tf_op jit(solution)/shard_map/pallas_call | solution.py:199
  119.4 0.0 copy-start
  119.4 0.0 copy-start.1
  119.4 0.0 copy-start.2
  119.4 42.6 %all-gather.2.cloned.1.call-done = bf16[1,2048,4096]{2,1,0:T(8,128)(2,1)} async-done(((bf16[1,128,4096]{2,1,0:T(8,128)(2,1)}), bf16[1,2048,4096]{2,1,0:T(8,128)(2,1)}) %all-gather.2.cloned.1.call-update) | async-done | bytes 16777232 | tf_op jit(solution)/shard_map/all_gather | solution.py:226
  162.0 0.0 copy-start.8
  162.0 10.3 %fusion.21 = bf16[1,4096,256]{1,2,0:T(8,128)(2,1)S(1)} fusion(bf16[2048,256]{1,0:T(8,128)(2,1)S(1)} %get-tuple-element.18.refs_0_, bf16[1,2048,4096]{2,1,0:T(8,128)(2,1)} %all-gather.2.cloned.1.call-done), kind=kOutput, calls=%fused_computation.12 | convolution fusion | flops 4296015872 | bytes 19922944 | tf_op jit(solution)/shard_map/dot_general | solution.py:233
  172.3 0.0 copy-done
  172.3 0.0 copy-done.1
  172.3 0.2 copy-done.8
  172.5 4.7 %fusion.18 = bf16[1,4096,256]{1,2,0:T(8,128)(2,1)S(1)} fusion(bf16[2048,256]{1,0:T(8,128)(2,1)S(1)} %get-tuple-element.19.refs_1_, bf16[1,2048,4096]{2,1,0:T(8,128)(2,1)S(1)} %copy-done.8), kind=kOutput, calls=%fused_computation.11 | convolution fusion | flops 4296015872 | bytes 19922944 | tf_op jit(solution)/shard_map/dot_general | solution.py:233
  177.3 0.0 copy-done.2
  177.3 4.8 %fusion.15 = bf16[1,4096,256]{1,2,0:T(8,128)(2,1)S(1)} fusion(bf16[2048,256]{1,0:T(8,128)(2,1)S(1)} %get-tuple-element.20.refs_2_, bf16[1,2048,4096]{2,1,0:T(8,128)(2,1)S(1)} %copy-done.8), kind=kOutput, calls=%fused_computation.10 | convolution fusion | flops 4296015872 | bytes 19922944 | tf_op jit(solution)/shard_map/dot_general | solution.py:233
  182.1 3.1 %pad_maximum_fusion = bf16[3,4096,256]{1,2,0:T(8,128)(2,1)} fusion(bf16[1,4096,256]{1,2,0:T(8,128)(2,1)S(1)} %fusion.15, bf16[1,4096,256]{1,2,0:T(8,128)(2,1)S(1)} %fusion.18, bf16[1,4096,256]{1,2,0:T(8,128)(2,1)S(1)} %fusion.21), kind=kLoop, calls=%fused_computation.6 | loop fusion | flops 6291456 | bytes 12582912 | tf_op jit(solution)/shard_map/stack | solution.py:235
  185.2 0.0 reduce-scatter.2.cloned.1.call-update
  185.2 46.2 %shard_map.104 = (bf16[128,4096]{1,0:T(8,128)(2,1)}, bf16[128,4096]{1,0:T(8,128)(2,1)}, bf16[128,4096]{1,0:T(8,128)(2,1)}) custom-call(bf16[2048,256]{1,0:T(8,128)(2,1)} %copy-done, bf16[2048,256]{1,0:T(8,128)(2,1)} %copy-done.1, bf16[2048,256]{1,0:T(8,128)(2,1)} %copy-done.2), custom_call_target="tpu_custom_call" | custom-call | bytes 50331648 | tf_op jit(solution)/shard_map/pallas_call | solution.py:104
  231.4 0.0 reduce-scatter.2.cloned.1.call-done
  231.5 1.3 convert_multiply_fusion
  232.8 0.0 copy-start.9
  232.8 1.6 copy.12
  234.4 2.3 copy.16
  236.7 2.3 copy.17
  239.0 0.0 copy-done.9
  239.0 1.0 copy.18
Async XLA Ops:
  7.2 80.0 %copy-start.7 = (s32[1,16]{1,0:T(1,128)S(1)}, s32[1,16]{1,0:T(1,128)}, u32[]{:S(2)}) copy-start(s32[1,16]{1,0:T(1,128)} %param.13) | copy-start | bytes 196
  7.2 154.8 %all-gather.2.cloned.1.call-start = ((), (), s32[]{:S(2)}) async-start(), calls=%async_computation.1 | async-start | bytes 17825792 | tf_op jit(solution)/shard_map/all_gather | solution.py:226
  7.9 223.6 %reduce-scatter.2.cloned.1.call-start = ((), (), s32[]{:S(2)}) async-start(), calls=%async_computation.2 | async-start | bytes 7077888 | tf_op jit(solution)/shard_map/reduce_scatter | solution.py:236
  87.2 1.2 copy-start.3
  88.4 1.2 copy-start.4
  89.6 1.2 copy-start.5
  90.9 1.5 copy-start.6
  119.4 52.9 %copy-start = (bf16[2048,256]{1,0:T(8,128)(2,1)}, bf16[2048,256]{1,0:T(8,128)(2,1)S(1)}, u32[]{:S(2)}) copy-start(bf16[2048,256]{1,0:T(8,128)(2,1)S(1)} %get-tuple-element.18.refs_0_) | copy-start | bytes 3145732
  119.4 52.9 %copy-start.1 = (bf16[2048,256]{1,0:T(8,128)(2,1)}, bf16[2048,256]{1,0:T(8,128)(2,1)S(1)}, u32[]{:S(2)}) copy-start(bf16[2048,256]{1,0:T(8,128)(2,1)S(1)} %get-tuple-element.19.refs_1_) | copy-start | bytes 3145732
  119.4 57.9 %copy-start.2 = (bf16[2048,256]{1,0:T(8,128)(2,1)}, bf16[2048,256]{1,0:T(8,128)(2,1)S(1)}, u32[]{:S(2)}) copy-start(bf16[2048,256]{1,0:T(8,128)(2,1)S(1)} %get-tuple-element.20.refs_2_) | copy-start | bytes 3145732
  162.0 10.5 %copy-start.8 = (bf16[1,2048,4096]{2,1,0:T(8,128)(2,1)S(1)}, bf16[1,2048,4096]{2,1,0:T(8,128)(2,1)}, u32[]{:S(2)}) copy-start(bf16[1,2048,4096]{2,1,0:T(8,128)(2,1)} %all-gather.2.cloned.1.call-done) | copy-start | bytes 50331652
  232.8 6.2 %copy-start.9 = (bf16[128,4096]{1,0:T(8,128)(2,1)S(1)}, bf16[128,4096]{1,0:T(8,128)(2,1)}, u32[]{:S(2)}) copy-start(bf16[128,4096]{1,0:T(8,128)(2,1)} %get-tuple-element.23) | copy-start | bytes 3145732
Sparse Core Ops, SparseCore 0:
  10.2 151.7 all-gather.1
  185.3 41.4 reduce-scatter.1

commit v2 on v1

--- a/solution.py
+++ b/solution.py
@@ -18,40 +18,42 @@
 MESH = pl.DeviceIdType.MESH
 
 
-def offsets():
-    pairs = [(dx, dz) for dx in range(SIDE) for dz in range(SIDE) if dx or dz]
-    far = lambda d: min(d, SIDE - d)
-    return sorted(pairs, key=lambda p: -(far(p[0]) + far(p[1])))
-
-
-def peer_of(me, dx, dz):
-    x, z = me // SIDE, lax.rem(me, SIDE)
-    return lax.rem(x + dx, SIDE) * SIDE + lax.rem(z + dz, SIDE)
-
-
-def greet(me):
+OFFSETS = (
+    (2, 2), (2, 1), (2, 3), (1, 2), (3, 2), (2, 0), (0, 2), (1, 1),
+    (3, 3), (1, 3), (3, 1), (1, 0), (3, 0), (0, 1), (0, 3),
+)
+
+
+def peer_of(offset):
+    me, core = lax.axis_index("seq"), lax.rem(lax.axis_index("dp"), 2)
+    place = []
+    for at, step in zip((me // SIDE, lax.rem(me, SIDE)), offset):
+        back = (SIDE - step) % SIDE
+        place.append(lax.rem(at + step + core * (back - step), SIDE))
+    return place[0] * SIDE + place[1]
+
+
+def block(index, size):
+    return pl.ds(pl.multiple_of(index * size, size), size)
+
+
+def to_heads(*refs):
+    ins, outs = refs[:4], refs[4:8]
+    send_sem, recv_sem, own_sem = refs[8:]
+    me = lax.axis_index("seq")
     barrier = pltpu.get_barrier_semaphore()
-    for dx, dz in offsets():
+    for offset in OFFSETS:
         pl.semaphore_signal(
-            barrier, inc=1, device_id={"seq": peer_of(me, dx, dz)}, device_id_type=MESH
+            barrier, inc=1, device_id={"seq": peer_of(offset)}, device_id_type=MESH
         )
     pl.semaphore_wait(barrier, SEQ - 1)
-
-
-def to_heads_kernel(count, *refs):
-    ins, outs = refs[:count], refs[count : 2 * count]
-    send_sem, recv_sem, own_sem = refs[2 * count :]
-    me = lax.axis_index("seq")
-    greet(me)
-    rows = pl.ds(pl.multiple_of(me * BLK, BLK), BLK)
     copies = []
-    for i, (dx, dz) in enumerate(offsets()):
-        peer = peer_of(me, dx, dz)
-        cols = pl.ds(pl.multiple_of(peer * COLS, COLS), COLS)
-        for a in range(count):
+    for a in range(4):
+        for i, offset in enumerate(OFFSETS):
+            peer = peer_of(offset)
             copy = pltpu.make_async_remote_copy(
-                src_ref=ins[a].at[:, cols],
-                dst_ref=outs[a].at[rows, :],
+                src_ref=ins[a].at[:, block(peer, COLS)],
+                dst_ref=outs[a].at[block(me, BLK), :],
                 send_sem=send_sem.at[a, i],
                 recv_sem=recv_sem.at[a, i],
                 device_id={"seq": peer},
@@ -59,63 +61,229 @@
             )
             copy.start()
             copies.append(copy)
-    mine = pl.ds(pl.multiple_of(me * COLS, COLS), COLS)
-    for a in range(count):
-        own = pltpu.make_async_copy(ins[a].at[:, mine], outs[a].at[rows, :], own_sem.at[a])
+    for a in range(4):
+        own = pltpu.make_async_copy(
+            ins[a].at[:, block(me, COLS)], outs[a].at[block(me, BLK), :], own_sem.at[a]
+        )
         own.start()
         copies.append(own)
     for copy in copies:
         copy.wait()
 
 
-def to_rows_kernel(count, *refs):
-    ins, outs = refs[:count], refs[count : 2 * count]
-    send_sem, recv_sem, own_sem = refs[2 * count :]
-    me = lax.axis_index("seq")
-    greet(me)
-    mine = pl.ds(pl.multiple_of(me * COLS, COLS), COLS)
-    copies = []
-    for i, (dx, dz) in enumerate(offsets()):
-        peer = peer_of(me, dx, dz)
-        rows = pl.ds(pl.multiple_of(peer * BLK, BLK), BLK)
-        for a in range(count):
-            copy = pltpu.make_async_remote_copy(
-                src_ref=ins[a].at[rows, :],
-                dst_ref=outs[a].at[:, mine],
-                send_sem=send_sem.at[a, i],
-                recv_sem=recv_sem.at[a, i],
-                device_id={"seq": peer},
-                device_id_type=MESH,
-            )
-            copy.start()
-            copies.append(copy)
-    rows = pl.ds(pl.multiple_of(me * BLK, BLK), BLK)
-    for a in range(count):
-        own = pltpu.make_async_copy(ins[a].at[rows, :], outs[a].at[:, mine], own_sem.at[a])
-        own.start()
-        copies.append(own)
-    for copy in copies:
-        copy.wait()
-
-
-def exchange(kernel, arrays, shape, collective_id):
-    count = len(arrays)
-    moved = count * SEQ * BLK * COLS * 2
+def heads_exchange(arrays):
+    tokens = SEQ * BLK
     return pl.pallas_call(
-        functools.partial(kernel, count),
-        out_shape=[jax.ShapeDtypeStruct(shape, jnp.bfloat16)] * count,
-        in_specs=[pl.BlockSpec(memory_space=pl.ANY)] * count,
-        out_specs=[pl.BlockSpec(memory_space=pl.ANY)] * count,
+        to_heads,
+        out_shape=[jax.ShapeDtypeStruct((tokens, COLS), jnp.bfloat16)] * 4,
+        in_specs=[pl.BlockSpec(memory_space=pl.ANY)] * 4,
+        out_specs=[pl.BlockSpec(memory_space=pltpu.VMEM)] * 4,
         scratch_shapes=[
-            pltpu.SemaphoreType.DMA((count, SEQ - 1)),
-            pltpu.SemaphoreType.DMA((count, SEQ - 1)),
-            pltpu.SemaphoreType.DMA((count,)),
+            pltpu.SemaphoreType.DMA((4, SEQ - 1)),
+            pltpu.SemaphoreType.DMA((4, SEQ - 1)),
+            pltpu.SemaphoreType.DMA((4,)),
         ],
         compiler_params=pltpu.CompilerParams(
-            collective_id=collective_id, has_side_effects=True
+            collective_id=0, has_side_effects=True, vmem_limit_bytes=16 << 20
         ),
-        cost_estimate=pl.CostEstimate(flops=0, bytes_accessed=16 * moved, transcendentals=0),
     )(*arrays)
+
+
+STRIPS = 4
+STRIP = 1024
+TURNS = (2, 1, 3, 0)
+WIDE = 3 * COLS
+PIECE = 512
+
+
+def finish(x_ref, dq_ref, dk_ref, dv_ref, qg_ref, kg_ref, vg_ref, w_ref,
+           xg, gt, keep, sib_out, sib_in, y_out, y_in,
+           load_sem, ring_send, ring_recv, back_send, back_recv, own_sem, sib_sem, y_sem):
+    me, dp = lax.axis_index("seq"), lax.axis_index("dp")
+    x, z, y, core = me // SIDE, lax.rem(me, SIDE), dp // 2, lax.rem(dp, 2)
+    turn = lambda at, by: lax.rem(at + by, SIDE)
+    f32 = jnp.float32
+    grads, homes = (dq_ref, dk_ref, dv_ref), (qg_ref, kg_ref, vg_ref)
+
+    loads = []
+    for k in range(STRIPS):
+        load = pltpu.make_async_copy(
+            x_ref.at[:, block(turn(y, TURNS[k]), STRIP)], xg.at[k, x, z], load_sem.at[k]
+        )
+        load.start()
+        loads.append(load)
+    barrier = pltpu.get_barrier_semaphore()
+    friends = [(peer_of(offset), dp) for offset in OFFSETS]
+    friends += [(me, y * 2 + 1 - core)]
+    friends += [(me, turn(y, by) * 2 + core) for by in (1, 2, 3)]
+    for friend in friends:
+        pl.semaphore_signal(barrier, inc=1, device_id=friend, device_id_type=MESH)
+    pl.semaphore_wait(barrier, len(friends))
+
+    started = []
+
+    def send(src, dst, sems, device):
+        copy = pltpu.make_async_remote_copy(
+            src_ref=src, dst_ref=dst, send_sem=sems[0], recv_sem=sems[1],
+            device_id=device, device_id_type=MESH,
+        )
+        copy.start()
+        started.append(copy)
+        return copy
+
+    def ring(k, part, stage):
+        cols = slice(part * (STRIP // 2), (part + 1) * (STRIP // 2))
+        along_x = (part == 0) == (stage < 2)
+        copies = []
+        for way, step in enumerate((1, 3)):
+            owner = 0 if stage % 2 == 0 else SIDE - step
+            rows = slice(0, BLK) if stage % 2 == 0 else slice(way * (BLK // 2), (way + 1) * (BLK // 2))
+            if along_x:
+                device = (turn(x, step) * SIDE + z, dp)
+                group = (turn(x, owner), z if stage < 2 else slice(None))
+            else:
+                device = (x * SIDE + turn(z, step), dp)
+                group = (x if stage < 2 else slice(None), turn(z, owner))
+            place = xg.at[k, group[0], group[1], rows, cols]
+            at = ((k * 2 + part) * 4 + stage) * 2 + way
+            copies.append(send(place, place, (ring_send.at[at], ring_recv.at[at]), device))
+        return copies
+
+    flights = {}
+
+    def advance(k, stage):
+        for part in (0, 1):
+            if stage == 0 and part == 0:
+                loads[k].wait()
+            if stage > 0:
+                for copy in flights[k, part, stage - 1]:
+                    copy.wait_recv()
+            if stage < 4:
+                flights[k, part, stage] = ring(k, part, stage)
+
+    homeward = []
+
+    def go_home(a):
+        for i, offset in enumerate(OFFSETS):
+            peer = peer_of(offset)
+            homeward.append(send(
+                grads[a].at[block(peer, BLK), :], homes[a].at[:, block(me, COLS)],
+                (back_send.at[a, i], back_recv.at[a, i]), (peer, dp),
+            ))
+        own = pltpu.make_async_copy(
+            grads[a].at[block(me, BLK), :], homes[a].at[:, block(me, COLS)], own_sem.at[a]
+        )
+        own.start()
+        owns.append(own)
+
+    owns, siblings, across = [], [], []
+
+    def product(k):
+        for half in (0, 1):
+            first = (1 - core if half == 0 else core) * PIECE
+
+            @pl.loop(0, PIECE // 256)
+            def _(tile):
+                cols = pl.ds(pl.multiple_of(first + tile * 256, 256), 256)
+                here = pl.ds(pl.multiple_of(tile * 256, 256), 256)
+                right = xg[k, :, :, :, cols].reshape(SEQ * BLK, 256)
+                value = jnp.dot(gt[...], right, preferred_element_type=f32)
+                if half == 0:
+                    sib_out[k, :, here] = value.astype(jnp.bfloat16)
+                else:
+                    keep[k % 2, :, here] = value
+
+            if half == 0:
+                siblings.append(send(
+                    sib_out.at[k], sib_in.at[k], (sib_sem.at[0, k], sib_sem.at[1, k]),
+                    (me, y * 2 + 1 - core),
+                ))
+
+    def settle(k):
+        siblings[k].wait_recv()
+        if k < STRIPS - 1:
+            y_out[k] = (keep[k % 2] + sib_in[k].astype(f32)).astype(jnp.bfloat16)
+            across.append(send(
+                y_out.at[k], y_in.at[k], (y_sem.at[0, k], y_sem.at[1, k]),
+                (me, turn(y, TURNS[k]) * 2 + core),
+            ))
+        else:
+            total = keep[k % 2] + sib_in[k].astype(f32)
+            for i, copy in enumerate(across):
+                copy.wait_recv()
+                total += y_in[i].astype(f32)
+            w_ref[...] = total
+
+    for k in range(STRIPS):
+        advance(k, 0)
+    go_home(0)
+    for k in range(STRIPS):
+        advance(k, 1)
+    advance(0, 2)
+    advance(1, 2)
+
+    @pl.loop(0, SEQ)
+    def _(n):
+        for a in range(3):
+            for h in range(2):
+                tile = grads[a][block(n, BLK), h * HDIM : (h + 1) * HDIM]
+                gt[a * COLS + h * HDIM : a * COLS + (h + 1) * HDIM, block(n, BLK)] = tile.T
+
+    for k in range(STRIPS):
+        advance(k, 3)
+        if k + 2 < STRIPS:
+            advance(k + 2, 2)
+        if k < 2:
+            go_home(k + 1)
+        if k >= 1:
+            advance(k - 1, 4)
+            product(k - 1)
+        if k >= 2:
+            settle(k - 2)
+    settle(STRIPS - 2)
+    advance(STRIPS - 1, 4)
+    product(STRIPS - 1)
+    settle(STRIPS - 1)
+    for copy in homeward:
+        copy.wait_recv()
+    for own in owns:
+        own.wait()
+    for copy in started:
+        copy.wait_send()
+
+
+def closing(layer_rows, dq, dk, dv):
+    tokens, width = SEQ * BLK, layer_rows.shape[1]
+    vmem, any_place = pl.BlockSpec(memory_space=pltpu.VMEM), pl.BlockSpec(memory_space=pl.ANY)
+    bf16, f32 = jnp.bfloat16, jnp.float32
+    rings = STRIPS * 16
+    return pl.pallas_call(
+        finish,
+        out_shape=[jax.ShapeDtypeStruct((BLK, width), bf16)] * 3
+        + [jax.ShapeDtypeStruct((WIDE, PIECE), f32)],
+        in_specs=[any_place, vmem, vmem, vmem],
+        out_specs=[any_place] * 3 + [vmem],
+        scratch_shapes=[
+            pltpu.VMEM((STRIPS, SIDE, SIDE, BLK, STRIP), bf16),
+            pltpu.VMEM((WIDE, tokens), bf16),
+            pltpu.VMEM((2, WIDE, PIECE), f32),
+            pltpu.VMEM((STRIPS, WIDE, PIECE), bf16),
+            pltpu.VMEM((STRIPS, WIDE, PIECE), bf16),
+            pltpu.VMEM((STRIPS - 1, WIDE, PIECE), bf16),
+            pltpu.VMEM((STRIPS - 1, WIDE, PIECE), bf16),
+            pltpu.SemaphoreType.DMA((STRIPS,)),
+            pltpu.SemaphoreType.DMA((rings,)),
+            pltpu.SemaphoreType.DMA((rings,)),
+            pltpu.SemaphoreType.DMA((3, SEQ - 1)),
+            pltpu.SemaphoreType.DMA((3, SEQ - 1)),
+            pltpu.SemaphoreType.DMA((3,)),
+            pltpu.SemaphoreType.DMA((2, STRIPS)),
+            pltpu.SemaphoreType.DMA((2, STRIPS - 1)),
+        ],
+        compiler_params=pltpu.CompilerParams(
+            collective_id=1, has_side_effects=True, vmem_limit_bytes=56 << 20
+        ),
+    )(layer_rows, dq, dk, dv)
 
 
 def attend(kv_links, tallies, q_ref, k_ref, v_ref, g_ref, dq_ref, dk_ref, dv_ref, wq, turned, acc, sp):
@@ -215,27 +383,12 @@
 
 
 def local(layer_input, query_rows, key_rows, value_rows, out_grad, neighbours, counts):
-    dp_count = lax.axis_size("dp")
-    tokens = NQB * BLK
-    q, k, v, g = exchange(
-        to_heads_kernel,
-        [query_rows[0], key_rows[0], value_rows[0], out_grad[0]],
-        (tokens, COLS),
-        0,
-    )
-    whole = lax.all_gather(layer_input, "seq", axis=1, tiled=True)
+    q, k, v, g = heads_exchange([query_rows[0], key_rows[0], value_rows[0], out_grad[0]])
     dq, dk, dv = attention(neighbours[0], counts[0], q, k, v, g)
-    width = query_rows.shape[2]
-    query_grad, key_grad, value_grad = exchange(
-        to_rows_kernel, [dq, dk, dv], (BLK, width), 1
-    )
-    terms = [
-        jnp.dot(whole[0].T, part, preferred_element_type=jnp.float32) for part in (dq, dk, dv)
-    ]
-    summed = jnp.stack(terms, axis=0).astype(jnp.bfloat16)
-    owned = lax.psum_scatter(summed, "dp", scatter_dimension=1, tiled=True).astype(jnp.float32)
-    norm_factor = 1.0 / math.sqrt(tokens * dp_count)
-    return query_grad[None], key_grad[None], value_grad[None], owned * norm_factor
+    query_grad, key_grad, value_grad, turned = closing(layer_input[0], dq, dk, dv)
+    norm_factor = 1.0 / math.sqrt(SEQ * BLK * lax.axis_size("dp"))
+    owned = turned.reshape(3, COLS, PIECE).transpose(0, 2, 1) * norm_factor
+    return query_grad[None], key_grad[None], value_grad[None], owned
 
 
 def solution(mesh):

time: 248 us -> 245 us (0.988)
  Pallas kernels: 152 us -> 228 us
  waiting for transfers between devices: 43.3 us -> 0 us
  matrix products: 19.8 us -> 0 us
  between operations: 14.2 us -> 0.7 us
  other arithmetic: 4.47 us -> 1.57 us
    pallas_call x2, Pallas kernels: 125 us -> 202 us  [the longest x1 147 us: closing(): pl.pallas_call(finish, out_shape=[jax.ShapeDtypeStruct((BLK, width), bf16...]
    all_gather x1 -> x0, waiting for transfers between devices: 42.6 us -> none  [local(): whole = lax.all_gather(layer_input, 'seq', axis=1, tiled=True)]
    dot_general x3 -> x0, matrix products: 19.8 us -> none  [local(): jnp.dot(whole[0].T, part, preferred_element_type=jnp.float32)]
    another operation x1 -> x0, other arithmetic: 3.13 us -> none  [local(): summed = jnp.stack(terms, axis=0).astype(jnp.bfloat16)]
    unnamed x24 -> x25, local copies, waits for them, and re-layouts: 12.6 us -> 12 us
  transfers between devices with their start and end apart: 2 -> 0, of which waited for: 1 -> 0; matrix products, arithmetic and copies ran while one was open for 0% -> 0% of each run, Pallas kernels for 61% -> 0%
where the time goes in v2:
time: 245 us; the launch traced here: 244 us
  Pallas kernels  228 us (93%)
  local copies, waits for them, and re-layouts  14.4 us (6%)
    pallas_call x1, Pallas kernels, closing(): pl.pallas_call(finish, out_shape=[jax.ShapeDtypeStruct((BLK, width), bf16...  147 us
    pallas_call x1, Pallas kernels, heads_exchange(): pl.pallas_call(to_heads, out_shape=[jax.ShapeDtypeStruct((tokens, COLS),...  55.1 us
    pallas_call x1, Pallas kernels, attention(): pl.pallas_call(attend, out_shape=[jax.ShapeDtypeStruct((tokens, COLS), jn...  25.9 us
    unnamed x25, local copies, waits for them, and re-layouts  12 us

profile of v2, /device:TPU:1, one launch (start us, length us, event | category | flops | bytes accessed | tf_op | source)
XLA Modules:
  0.0 244.4 jit_solution(12998580840696073174)
XLA Ops:
  0.6 0.8 copy.11.kv_links
  1.4 0.0 copy-start
  1.4 1.2 copy-done
  2.6 0.0 copy-start.1
  2.6 1.2 copy-done.1
  3.8 0.0 copy-start.2
  3.8 1.2 copy-done.2
  5.1 0.0 copy-start.3
  5.1 1.2 copy-done.3
  6.3 0.0 copy-start.7
  6.3 55.1 %shard_map.102 = (bf16[2048,256]{1,0:T(8,128)(2,1)S(1)}, bf16[2048,256]{1,0:T(8,128)(2,1)S(1)}, bf16[2048,256]{1,0:T(8,128)(2,1)S(1)}, bf16[2048,256]{1,0:T(8,128)(2,1)S(1)}) custom-call(bf16[128,4096]{1,0:T(8,128)(2,1)S(1)} %bitcast.12, bf16[128,4096]{1,0:T(8,128)(2,1)S(1)} %bitcast.13, bf16[128,4096]{1,0:T(8,128)(2,1)S(1)} %bitcast.14, ...), custom_call_target="tpu_custom_call" | custom-call | tf_op jit(solution)/shard_map/pallas_call | solution.py:76
  61.4 0.0 copy-done.7
  61.4 25.9 %shard_map.103 = (bf16[2048,256]{1,0:T(8,128)(2,1)S(1)}, bf16[2048,256]{1,0:T(8,128)(2,1)S(1)}, bf16[2048,256]{1,0:T(8,128)(2,1)S(1)}) custom-call(s32[16,8]{1,0:T(8,128)S(1)} %copy.11.kv_links, s32[16]{0:T(128)S(1)} %bitcast.16, bf16[2048,256]{1,0:T(8,128)(2,1)S(1)} %get-tuple-element.15.q_ref, bf16[2048,256]{1,0:T(8,128)(2,1)S(1)} %get-tuple-element.16.k_ref, ...), custom_call_target="tpu_custom_call" | custom-call | flops 5368709120 | bytes 7340032 | tf_op jit(solution)/shard_map/pallas_call | solution.py:367
  87.3 0.0 copy-start.4
  87.3 1.0 copy-done.4
  88.2 0.0 copy-start.5
  88.2 1.0 copy-done.5
  89.2 0.0 copy-start.6
  89.2 1.0 copy-done.6
  90.2 146.9 %shard_map.104 = (bf16[128,4096]{1,0:T(8,128)(2,1)}, bf16[128,4096]{1,0:T(8,128)(2,1)}, bf16[128,4096]{1,0:T(8,128)(2,1)}, f32[768,512]{1,0:T(8,128)}) custom-call(bf16[128,4096]{1,0:T(8,128)(2,1)} %bitcast.22, bf16[2048,256]{1,0:T(8,128)(2,1)} %copy-done.4, bf16[2048,256]{1,0:T(8,128)(2,1)} %copy-done.5, bf16[2048,256]{1,0:T(8,128)(2,1)} %copy-done.6), custom_call_target="tpu_custom_call" | custom-call | tf_op jit(solution)/shard_map/pallas_call | solution.py:260
  237.0 1.6 broadcast_multiply_fusion
  238.6 0.0 copy-start.10
  238.6 1.6 copy.12
  240.2 0.0 copy-start.9
  240.2 0.0 copy-done.10
  240.2 1.0 copy.16
  241.2 0.6 copy-done.9
  241.8 0.0 copy-start.8
  241.8 1.0 copy.17
  242.8 0.6 copy-done.8
  243.4 1.0 copy.18
Async XLA Ops:
  1.4 1.2 copy-start
  2.6 1.2 copy-start.1
  3.8 1.2 copy-start.2
  5.1 1.2 copy-start.3
  6.3 55.1 %copy-start.7 = (s32[1,16]{1,0:T(1,128)S(1)}, s32[1,16]{1,0:T(1,128)}, u32[]{:S(2)}) copy-start(s32[1,16]{1,0:T(1,128)} %param.13) | copy-start | bytes 196
  87.3 1.0 copy-start.4
  88.2 1.0 copy-start.5
  89.2 1.0 copy-start.6
  238.6 1.6 copy-start.10
  240.2 1.6 copy-start.9
  241.8 1.6 copy-start.8

commit v3 on v2

v3 whole, which is shorter than its diff:
```python
import functools
import math

import jax
import jax.numpy as jnp
from jax import lax
from jax.experimental import pallas as pl
from jax.experimental.pallas import tpu as pltpu
from jax.sharding import PartitionSpec as P

HDIM = 128
BLK = 128
MAXNB = 8
NQB = 16
SEQ = 16
SIDE = 4
COLS = 256
LOG2E = 1.4426950408889634
MESH = pl.DeviceIdType.MESH


OFFSETS = (
    (2, 2), (2, 1), (2, 3), (1, 2), (3, 2), (2, 0), (0, 2), (1, 1),
    (3, 3), (1, 3), (3, 1), (1, 0), (3, 0), (0, 1), (0, 3),
)


def peer_of(offset):
    me, core = lax.axis_index("seq"), lax.rem(lax.axis_index("dp"), 2)
    place = []
    for at, step in zip((me // SIDE, lax.rem(me, SIDE)), offset):
        back = (SIDE - step) % SIDE
        place.append(lax.rem(at + step + core * (back - step), SIDE))
    return place[0] * SIDE + place[1]


def block(index, size):
    return pl.ds(pl.multiple_of(index * size, size), size)


def to_heads(*refs):
    ins, outs = refs[:4], refs[4:8]
    send_sem, recv_sem, own_sem = refs[8:]
    me = lax.axis_index("seq")
    barrier = pltpu.get_barrier_semaphore()
    for offset in OFFSETS:
        pl.semaphore_signal(
            barrier, inc=1, device_id={"seq": peer_of(offset)}, device_id_type=MESH
        )
    pl.semaphore_wait(barrier, SEQ - 1)
    copies = []
    for a in range(4):
        for i, offset in enumerate(OFFSETS):
            peer = peer_of(offset)
            copy = pltpu.make_async_remote_copy(
                src_ref=ins[a].at[:, block(peer, COLS)],
                dst_ref=outs[a].at[block(me, BLK), :],
                send_sem=send_sem.at[a, i],
                recv_sem=recv_sem.at[a, i],
                device_id={"seq": peer},
                device_id_type=MESH,
            )
            copy.start()
            copies.append(copy)
    for a in range(4):
        own = pltpu.make_async_copy(
            ins[a].at[:, block(me, COLS)], outs[a].at[block(me, BLK), :], own_sem.at[a]
        )
        own.start()
        copies.append(own)
    for copy in copies:
        copy.wait()


def heads_exchange(arrays):
    tokens = SEQ * BLK
    return pl.pallas_call(
        to_heads,
        out_shape=[jax.ShapeDtypeStruct((tokens, COLS), jnp.bfloat16)] * 4,
        in_specs=[pl.BlockSpec(memory_space=pltpu.HBM)] * 4,
        out_specs=[pl.BlockSpec(memory_space=pltpu.VMEM)] * 4,
        scratch_shapes=[
            pltpu.SemaphoreType.DMA((4, SEQ - 1)),
            pltpu.SemaphoreType.DMA((4, SEQ - 1)),
            pltpu.SemaphoreType.DMA((4,)),
        ],
        compiler_params=pltpu.CompilerParams(
            collective_id=0, has_side_effects=True, vmem_limit_bytes=58_500_000
        ),
    )(*arrays)


UNITS = 8
EARLY = 4
PIECE = 256
TURNS = (2, 2, 1, 1, 3, 3, 0, 0)
WIDE = 3 * COLS


def turn(at, by):
    return lax.rem(at + by, SIDE)


def finish(norm_factor, x_ref, early_ref, dq_ref, dk_ref, dv_ref, qg_ref, kg_ref, vg_ref, w_ref,
           xg, gt, prod, sib_in, y_out, y_in,
           load_sem, ring_send, ring_recv, back_send, back_recv, own_sem, sib_sem, y_sem):
    me, dp = lax.axis_index("seq"), lax.axis_index("dp")
    x, z, y, core = me // SIDE, lax.rem(me, SIDE), dp // 2, lax.rem(dp, 2)
    f32 = jnp.float32
    grads, homes = (dq_ref, dk_ref, dv_ref), (qg_ref, kg_ref, vg_ref)

    loads = {}
    for u in [*range(EARLY, UNITS), *range(EARLY)]:
        for part in (0, 1):
            spot = part * 2 + u % 2
            cols = slice(part * PIECE, (part + 1) * PIECE)
            if u < EARLY:
                at = (u // 2 * 4 + spot) * PIECE
                source, place = early_ref.at[:, :, :, at : at + PIECE], xg.at[u, :, :, :, cols]
            else:
                source = x_ref.at[:, block(turn(y, TURNS[u]) * 4 + spot, PIECE)]
                place = xg.at[u, x, z, :, cols]
            loads[u, part] = pltpu.make_async_copy(source, place, load_sem.at[u, part])
            loads[u, part].start()
    barrier = pltpu.get_barrier_semaphore()
    friends = [(peer_of(offset), dp) for offset in OFFSETS]
    friends += [(me, y * 2 + 1 - core)]
    friends += [(me, turn(y, by) * 2 + core) for by in (1, 2, 3)]
    for friend in friends:
        pl.semaphore_signal(barrier, inc=1, device_id=friend, device_id_type=MESH)
    pl.semaphore_wait(barrier, len(friends))

    started = []

    def send(src, dst, sems, device):
        copy = pltpu.make_async_remote_copy(
            src_ref=src, dst_ref=dst, send_sem=sems[0], recv_sem=sems[1],
            device_id=device, device_id_type=MESH,
        )
        copy.start()
        started.append(copy)
        return copy

    def ring(u, part, stage):
        cols = slice(part * PIECE, (part + 1) * PIECE)
        along_x = (part == 0) == (stage < 2)
        copies = []
        for way, step in enumerate((1, 3)):
            owner = 0 if stage % 2 == 0 else SIDE - step
            rows = slice(0, BLK) if stage % 2 == 0 else slice(way * (BLK // 2), (way + 1) * (BLK // 2))
            if along_x:
                device = (turn(x, step) * SIDE + z, dp)
                group = (turn(x, owner), z if stage < 2 else slice(None))
            else:
                device = (x * SIDE + turn(z, step), dp)
                group = (x if stage < 2 else slice(None), turn(z, owner))
            place = xg.at[u, group[0], group[1], rows, cols]
            at = (((u - EARLY) * 2 + part) * 4 + stage) * 2 + way
            copies.append(send(place, place, (ring_send.at[at], ring_recv.at[at]), device))
        return copies

    flights = {}

    def advance(u, stage):
        for part in (0, 1):
            if stage == 0:
                loads[u, part].wait()
            else:
                for copy in flights[u, part, stage - 1]:
                    copy.wait_recv()
            if stage < 4:
                flights[u, part, stage] = ring(u, part, stage)

    homeward, owns, siblings, across = [], [], {}, {}

    def go_home(a):
        for i, offset in enumerate(OFFSETS):
            peer = peer_of(offset)
            homeward.append(send(
                grads[a].at[block(peer, BLK), :], homes[a].at[:, block(me, COLS)],
                (back_send.at[a, i], back_recv.at[a, i]), (peer, dp),
            ))
        own = pltpu.make_async_copy(
            grads[a].at[block(me, BLK), :], homes[a].at[:, block(me, COLS)], own_sem.at[a]
        )
        own.start()
        owns.append(own)

    def product(u):
        @pl.loop(0, 2)
        def _(half):
            cols = block(lax.rem(1 - core + half, 2), PIECE)
            right = xg[u, :, :, :, cols].reshape(SEQ * BLK, PIECE)
            prod[u, half] = jnp.dot(gt[...], right, preferred_element_type=f32).astype(jnp.bfloat16)

        siblings[u] = send(
            prod.at[u, 0], sib_in.at[u], (sib_sem.at[0, u], sib_sem.at[1, u]),
            (me, y * 2 + 1 - core),
        )

    def settle(u):
        siblings[u].wait_recv()
        total = prod[u, 1].astype(f32) + sib_in[u].astype(f32)
        if u < UNITS - 2:
            y_out[u] = total.astype(jnp.bfloat16)
            across[u] = send(
                y_out.at[u], y_in.at[u], (y_sem.at[0, u], y_sem.at[1, u]),
                (me, turn(y, TURNS[u]) * 2 + core),
            )
        else:
            for i in range(u % 2, UNITS - 2, 2):
                across[i].wait_recv()
                total += y_in[i].astype(f32)
            for a in range(3):
                for h in range(2):
                    rows = slice(a * COLS + h * HDIM, a * COLS + (h + 1) * HDIM)
                    w_ref[a, (u % 2) * PIECE : (u % 2 + 1) * PIECE, h * HDIM : (h + 1) * HDIM] = (
                        total[rows].T * norm_factor
                    )

    late = range(EARLY, UNITS)
    for u in late:
        advance(u, 0)
    go_home(0)
    for u in late:
        advance(u, 1)
    for u in late:
        advance(u, 2)

    @pl.loop(0, SEQ)
    def _(n):
        for a in range(3):
            for h in range(2):
                tile = grads[a][block(n, BLK), h * HDIM : (h + 1) * HDIM]
                gt[a * COLS + h * HDIM : a * COLS + (h + 1) * HDIM, block(n, BLK)] = tile.T

    for u in range(EARLY):
        for part in (0, 1):
            loads[u, part].wait()
        product(u)
        if u >= 1:
            settle(u - 1)
    advance(EARLY, 3)
    if EARLY:
        settle(EARLY - 1)
    go_home(1)
    for u in late:
        if u + 1 < UNITS:
            advance(u + 1, 3)
        if u == UNITS - 2:
            go_home(2)
        advance(u, 4)
        product(u)
        settle(u)
    for copy in homeward:
        copy.wait_recv()
    for own in owns:
        own.wait()
    for copy in started:
        copy.wait_send()


def closing(norm_factor, layer_rows, early, dq, dk, dv):
    tokens, width = SEQ * BLK, layer_rows.shape[1]
    vmem, hbm = pl.BlockSpec(memory_space=pltpu.VMEM), pl.BlockSpec(memory_space=pltpu.HBM)
    bf16, f32 = jnp.bfloat16, jnp.float32
    rings = (UNITS - EARLY) * 16
    return pl.pallas_call(
        functools.partial(finish, norm_factor),
        out_shape=[jax.ShapeDtypeStruct((BLK, width), bf16)] * 3
        + [jax.ShapeDtypeStruct((3, 2 * PIECE, COLS), f32)],
        in_specs=[hbm, hbm, vmem, vmem, vmem],
        out_specs=[vmem] * 4,
        scratch_shapes=[
            pltpu.VMEM((UNITS, SIDE, SIDE, BLK, 2 * PIECE), bf16),
            pltpu.VMEM((WIDE, tokens), bf16),
            pltpu.VMEM((UNITS, 2, WIDE, PIECE), bf16),
            pltpu.VMEM((UNITS, WIDE, PIECE), bf16),
            pltpu.VMEM((UNITS - 2, WIDE, PIECE), bf16),
            pltpu.VMEM((UNITS - 2, WIDE, PIECE), bf16),
            pltpu.SemaphoreType.DMA((UNITS, 2)),
            pltpu.SemaphoreType.DMA((rings,)),
            pltpu.SemaphoreType.DMA((rings,)),
            pltpu.SemaphoreType.DMA((3, SEQ - 1)),
            pltpu.SemaphoreType.DMA((3, SEQ - 1)),
            pltpu.SemaphoreType.DMA((3,)),
            pltpu.SemaphoreType.DMA((2, UNITS)),
            pltpu.SemaphoreType.DMA((2, UNITS - 2)),
        ],
        compiler_params=pltpu.CompilerParams(
            collective_id=1, has_side_effects=True, vmem_limit_bytes=40 << 20
        ),
    )(layer_rows, early, dq, dk, dv)


def attend(kv_links, tallies, q_ref, k_ref, v_ref, g_ref, dq_ref, dk_ref, dv_ref, wq, turned, acc, sp):
    scale = HDIM ** (-0.5)
    heads = COLS // HDIM
    f32 = jnp.float32
    acc[...] = jnp.zeros_like(acc)
    wq[...] = jnp.zeros_like(wq)

    @pl.loop(0, NQB)
    def _(n):
        rows = pl.ds(pl.multiple_of(n * BLK, BLK), BLK)
        for h in range(heads):
            turned[h, n] = k_ref[rows, h * HDIM : (h + 1) * HDIM].astype(f32).T.astype(jnp.bfloat16)

    @pl.loop(0, NQB)
    def _(b):
        mine = pl.ds(pl.multiple_of(b * BLK, BLK), BLK)
        tally = tallies[b]

        def variant(slots):
            spans = [slice(h * HDIM, (h + 1) * HDIM) for h in range(heads)]
            rows = [block(kv_links[b, j], BLK) for j in range(slots)]
            for h in range(heads):
                wq[h, :HDIM, :HDIM] = q_ref[mine, spans[h]]
                wq[h, HDIM:, HDIM:] = g_ref[mine, spans[h]]
            tops = [None] * heads
            for j in range(slots):
                for h in range(heads):
                    kv = jnp.concatenate([k_ref[rows[j], spans[h]], v_ref[rows[j], spans[h]]], axis=1)
                    pair = lax.dot_general(
                        kv, wq[h], (((1,), (1,)), ((), ())), preferred_element_type=f32
                    )
                    score = pair[:, :HDIM]
                    if j == slots - 1 and slots > 1:
                        score = jnp.where(j < tally, score, -jnp.inf)
                    sp[h, j, :, :HDIM] = score
                    sp[h, j, :, HDIM:] = pair[:, HDIM:]
                    here = jnp.max(score.reshape(BLK // 8, 8, BLK), axis=0)
                    tops[h] = here if j == 0 else jnp.maximum(tops[h], here)
            tops = [jnp.max(top, axis=0, keepdims=True) for top in tops]
            totals, dots = [0.0] * heads, [0.0] * heads
            for j in range(slots):
                for h in range(heads):
                    weight = jnp.exp2((sp[h, j, :, :HDIM] - tops[h]) * (scale * LOG2E))
                    sp[h, j, :, :HDIM] = weight
                    totals[h] += jnp.sum(weight.reshape(BLK // 8, 8, BLK), axis=0)
                    slopes = weight * sp[h, j, :, HDIM:]
                    dots[h] += jnp.sum(slopes.reshape(BLK // 8, 8, BLK), axis=0)
            inverses = [1.0 / jnp.sum(total, axis=0, keepdims=True) for total in totals]
            dots = [jnp.sum(dot, axis=0, keepdims=True) * inv for dot, inv in zip(dots, inverses)]
            dqs = [0.0] * heads
            for j in range(slots):
                for h in range(heads):
                    prob = sp[h, j, :, :HDIM] * inverses[h]
                    slope = (prob * (sp[h, j, :, HDIM:] - dots[h])).astype(jnp.bfloat16)
                    left = jnp.concatenate([slope, prob.astype(jnp.bfloat16)], axis=1)
                    acc[h, rows[j], :] += jnp.dot(left, wq[h], preferred_element_type=f32)
                    dqs[h] += jnp.dot(turned[h, kv_links[b, j]], slope, preferred_element_type=f32)
            for h in range(heads):
                dq_ref[mine, spans[h]] = (dqs[h].T * scale).astype(jnp.bfloat16)

        for slots in range(2, MAXNB + 1, 2):
            pl.when((tally == slots) | (tally == slots - 1))(functools.partial(variant, slots))

    @pl.loop(0, NQB)
    def _(n):
        rows = pl.ds(pl.multiple_of(n * BLK, BLK), BLK)
        for h in range(heads):
            cols = slice(h * HDIM, (h + 1) * HDIM)
            dk_ref[rows, cols] = (acc[h, rows, :HDIM] * scale).astype(jnp.bfloat16)
            dv_ref[rows, cols] = acc[h, rows, HDIM:].astype(jnp.bfloat16)


def attention(links, tallies, q, k, v, g):
    tokens = NQB * BLK
    heads = COLS // HDIM
    spec = pl.BlockSpec(memory_space=pltpu.VMEM)
    smem = pl.BlockSpec(memory_space=pltpu.SMEM)
    flops = heads * NQB * MAXNB * 5 * 2 * BLK**3
    return pl.pallas_call(
        attend,
        out_shape=[jax.ShapeDtypeStruct((tokens, COLS), jnp.bfloat16)] * 3,
        in_specs=[smem, smem] + [spec] * 4,
        out_specs=[spec] * 3,
        scratch_shapes=[
            pltpu.VMEM((heads, 2 * HDIM, 2 * BLK), jnp.bfloat16),
            pltpu.VMEM((heads, NQB, HDIM, BLK), jnp.bfloat16),
            pltpu.VMEM((heads, tokens, 2 * HDIM), jnp.float32),
            pltpu.VMEM((heads, MAXNB, BLK, 2 * BLK), jnp.float32),
        ],
        compiler_params=pltpu.CompilerParams(vmem_limit_bytes=16 << 20),
        cost_estimate=pl.CostEstimate(
            flops=flops, bytes_accessed=7 * tokens * COLS * 2, transcendentals=heads * NQB * MAXNB * BLK * BLK
        ),
    )(links, tallies, q, k, v, g)


def gather_early(layer_rows):
    y = lax.axis_index("dp") // 2
    width = 4 * PIECE
    parts = [
        lax.dynamic_slice_in_dim(layer_rows, turn(y, TURNS[u]) * width, width, 1)
        for u in range(0, EARLY, 2)
    ]
    mine = jnp.concatenate(parts, axis=1)
    whole = lax.all_gather(mine[None], "seq", axis=1, tiled=True)
    return whole.reshape(SIDE, SIDE, BLK, EARLY // 2 * width)


def local(layer_input, query_rows, key_rows, value_rows, out_grad, neighbours, counts):
    early = gather_early(layer_input[0])
    q, k, v, g = heads_exchange([query_rows[0], key_rows[0], value_rows[0], out_grad[0]])
    dq, dk, dv = attention(neighbours[0], counts[0], q, k, v, g)
    norm_factor = 1.0 / math.sqrt(SEQ * BLK * lax.axis_size("dp"))
    query_grad, key_grad, value_grad, owned = closing(norm_factor, layer_input[0], early, dq, dk, dv)
    return query_grad[None], key_grad[None], value_grad[None], owned


def solution(mesh):
    rows = P("dp", "seq", None)
    return jax.shard_map(
        local,
        mesh=mesh,
        in_specs=(rows,) * 5 + (P("dp", None, None), P("dp", None)),
        out_specs=(rows, rows, rows, P(None, "dp", "seq")),
        check_vma=False,
    )
```

time: 245 us -> 219 us (0.89)
  Pallas kernels: 228 us -> 173 us
  waiting for transfers between devices: 0 us -> 16.5 us
  between operations: 0.7 us -> 14.1 us
    pallas_call x1, Pallas kernels: 147 us -> 88.7 us  [closing(): pl.pallas_call(functools.partial(finish, norm_factor), out_shape=[jax.Sha...]
    all_gather x0 -> x1, waiting for transfers between devices: none -> 16.5 us  [gather_early(): whole = lax.all_gather(mine[None], 'seq', axis=1, tiled=True)]
    pallas_call x1, Pallas kernels: 55.1 us -> 65.7 us  [heads_exchange(): pl.pallas_call(to_heads, out_shape=[jax.ShapeDtypeStruct((tokens, COLS),...]
    pallas_call x1, Pallas kernels: 25.9 us -> 18.4 us  [attention(): pl.pallas_call(attend, out_shape=[jax.ShapeDtypeStruct((tokens, COLS), jn...]
    unnamed x25 -> x22, local copies, waits for them, and re-layouts: 12 us -> 11.5 us
  transfers between devices with their start and end apart: 0 -> 1, of which waited for: 0 -> 1; matrix products, arithmetic and copies ran while one was open for 0% -> 0% of each run, Pallas kernels for 0% -> 39%
where the time goes in v3:
time: 219 us; the launch traced here: 217 us
  Pallas kernels  173 us (79%)
  waiting for transfers between devices  16.5 us (8%)
  between operations  14.1 us (6%)
  local copies, waits for them, and re-layouts  12.6 us (6%)
    pallas_call x1, Pallas kernels, closing(): pl.pallas_call(functools.partial(finish, norm_factor), out_shape=[jax.Sha...  88.7 us
    pallas_call x1, Pallas kernels, heads_exchange(): pl.pallas_call(to_heads, out_shape=[jax.ShapeDtypeStruct((tokens, COLS),...  65.7 us
    pallas_call x1, Pallas kernels, attention(): pl.pallas_call(attend, out_shape=[jax.ShapeDtypeStruct((tokens, COLS), jn...  18.4 us
    all_gather x1, waiting for transfers between devices, gather_early(): whole = lax.all_gather(mine[None], 'seq', axis=1, tiled=True)  16.5 us
    unnamed x22, local copies, waits for them, and re-layouts  11.5 us
  transfers between devices with their start and end apart: 1, of which 1 were waited for; matrix products, arithmetic and copies ran while one was open for 0% of the time, Pallas kernels for 39%

profile of v3, /device:TPU:1, one launch (start us, length us, event | category | flops | bytes accessed | tf_op | source)
XLA Modules:
  0.0 216.9 jit_solution(9862462199535735583)
XLA Ops:
  7.2 0.0 copy-start.8
  7.2 0.0 all-gather.3.cloned.1.call-start
  7.3 1.1 dynamic-slice_bitcast_fusion.1
  8.3 0.8 pad_maximum_fusion
  9.2 0.0 all-gather.3.cloned.1.call-update
  9.2 0.0 copy-done.8
  9.2 0.1 copy.11.kv_links
  9.3 0.0 copy-start.7
  9.3 65.7 %shard_map.102 = (bf16[2048,256]{1,0:T(8,128)(2,1)}, bf16[2048,256]{1,0:T(8,128)(2,1)}, bf16[2048,256]{1,0:T(8,128)(2,1)}, bf16[2048,256]{1,0:T(8,128)(2,1)}) custom-call(bf16[128,4096]{1,0:T(8,128)(2,1)} %bitcast.21, bf16[128,4096]{1,0:T(8,128)(2,1)} %bitcast.22, bf16[128,4096]{1,0:T(8,128)(2,1)} %bitcast.23, bf16[128,4096]{1,0:T(8,128)(2,1)} %bitcast.24), custom_call_target="tpu_custom_call" | custom-call | tf_op jit(solution)/shard_map/pallas_call | solution.py:77
  74.9 0.0 copy-done.7
  74.9 0.0 copy-start.3
  75.0 1.2 copy-done.3
  76.2 0.0 copy-start.4
  76.2 1.2 copy-done.4
  77.4 0.0 copy-start.5
  77.4 1.2 copy-done.5
  78.6 0.0 copy-start.6
  78.6 1.5 copy-done.6
  80.2 0.0 copy-start
  80.2 18.4 %shard_map.103 = (bf16[2048,256]{1,0:T(8,128)(2,1)S(1)}, bf16[2048,256]{1,0:T(8,128)(2,1)S(1)}, bf16[2048,256]{1,0:T(8,128)(2,1)S(1)}) custom-call(s32[16,8]{1,0:T(8,128)S(1)} %copy.11.kv_links, s32[16]{0:T(128)S(1)} %bitcast.19, bf16[2048,256]{1,0:T(8,128)(2,1)S(1)} %copy-done.3, bf16[2048,256]{1,0:T(8,128)(2,1)S(1)} %copy-done.4, ...), custom_call_target="tpu_custom_call" | custom-call | flops 5368709120 | bytes 7340032 | tf_op jit(solution)/shard_map/pallas_call | solution.py:374
  98.6 0.0 copy-start.1
  98.6 1.0 copy-done.1
  99.6 16.5 %all-gather.3.cloned.1.call-done = bf16[2048,2048]{1,0:T(8,128)(2,1)} async-done(((bf16[128,2048]{1,0:T(8,128)(2,1)}), bf16[2048,2048]{1,0:T(8,128)(2,1)}) %all-gather.3.cloned.1.call-update) | async-done | bytes 8388624 | tf_op jit(solution)/shard_map/all_gather | solution.py:400
  116.1 0.0 copy-done
  116.1 0.0 copy-start.2
  116.1 1.2 copy-done.2
  117.3 88.7 %shard_map.104 = (bf16[128,4096]{1,0:T(8,128)(2,1)S(1)}, bf16[128,4096]{1,0:T(8,128)(2,1)S(1)}, bf16[128,4096]{1,0:T(8,128)(2,1)S(1)}, f32[3,512,256]{2,1,0:T(8,128)S(1)}) custom-call(bf16[128,4096]{1,0:T(8,128)(2,1)S(1)} %bitcast.15, bf16[4,4,128,2048]{3,2,1,0:T(8,128)(2,1)} %bitcast.20, bf16[2048,256]{1,0:T(8,128)(2,1)S(1)} %get-tuple-element.19.dq_ref, ...), custom_call_target="tpu_custom_call" | custom-call | tf_op jit(solution)/shard_map/pallas_call | solution.py:268
  206.0 1.0 copy.16
  207.0 1.0 copy.17
  208.0 1.0 copy.18
  208.9 1.1 copy.19
Async XLA Ops:
  7.2 2.0 copy-start.8
  7.2 108.9 %all-gather.3.cloned.1.call-start = ((), (), s32[]{:S(2)}) async-start(), calls=%async_computation | async-start | bytes 8912896 | tf_op jit(solution)/shard_map/all_gather | solution.py:400
  9.3 65.7 %copy-start.7 = (s32[1,16]{1,0:T(1,128)S(1)}, s32[1,16]{1,0:T(1,128)}, u32[]{:S(2)}) copy-start(s32[1,16]{1,0:T(1,128)} %param.13) | copy-start | bytes 196
  74.9 1.2 copy-start.3
  76.2 1.2 copy-start.4
  77.4 1.2 copy-start.5
  78.6 1.5 copy-start.6
  80.2 35.9 %copy-start = (bf16[1,128,4096]{2,1,0:T(8,128)(2,1)S(1)}, bf16[1,128,4096]{2,1,0:T(8,128)(2,1)}, u32[]{:S(2)}) copy-start(bf16[1,128,4096]{2,1,0:T(8,128)(2,1)} %param.7) | copy-start | bytes 3145732
  98.6 1.0 copy-start.1
  116.1 1.2 copy-start.2
Sparse Core Ops, SparseCore 0:
  10.7 105.3 all-gather.2

commit v4 on v3

--- a/solution.py
+++ b/solution.py
@@ -234,24 +234,28 @@
                 tile = grads[a][block(n, BLK), h * HDIM : (h + 1) * HDIM]
                 gt[a * COLS + h * HDIM : a * COLS + (h + 1) * HDIM, block(n, BLK)] = tile.T
 
+    ahead, leaving = EARLY, True
     for u in range(EARLY):
         for part in (0, 1):
             loads[u, part].wait()
         product(u)
-        if u >= 1:
+        advance(ahead, 3)
+        ahead += 1
+        if u:
             settle(u - 1)
-    advance(EARLY, 3)
-    if EARLY:
-        settle(EARLY - 1)
-    go_home(1)
+        if u == min(2, EARLY - 1):
+            go_home(1)
+    settle(EARLY - 1)
     for u in late:
-        if u + 1 < UNITS:
-            advance(u + 1, 3)
-        if u == UNITS - 2:
-            go_home(2)
+        if ahead < UNITS:
+            advance(ahead, 3)
+            ahead += 1
         advance(u, 4)
         product(u)
         settle(u)
+        if leaving and ahead == UNITS:
+            go_home(2)
+            leaving = False
     for copy in homeward:
         copy.wait_recv()
     for own in owns:
@@ -401,12 +405,34 @@
     return whole.reshape(SIDE, SIDE, BLK, EARLY // 2 * width)
 
 
+def hand_over(*refs):
+    ins, outs, sem = refs[:4], refs[4:8], refs[8]
+    copies = [pltpu.make_async_copy(a, b, sem.at[i]) for i, (a, b) in enumerate(zip(ins, outs))]
+    for copy in copies:
+        copy.start()
+    for copy in copies:
+        copy.wait()
+
+
+def settled(arrays):
+    return pl.pallas_call(
+        hand_over,
+        out_shape=[jax.ShapeDtypeStruct(a.shape, a.dtype) for a in arrays],
+        in_specs=[pl.BlockSpec(memory_space=pltpu.VMEM)] * 4,
+        out_specs=[pl.BlockSpec(memory_space=pltpu.HBM)] * 4,
+        scratch_shapes=[pltpu.SemaphoreType.DMA((4,))],
+        compiler_params=pltpu.CompilerParams(vmem_limit_bytes=8 << 20),
+    )(*arrays)
+
+
 def local(layer_input, query_rows, key_rows, value_rows, out_grad, neighbours, counts):
     early = gather_early(layer_input[0])
     q, k, v, g = heads_exchange([query_rows[0], key_rows[0], value_rows[0], out_grad[0]])
     dq, dk, dv = attention(neighbours[0], counts[0], q, k, v, g)
     norm_factor = 1.0 / math.sqrt(SEQ * BLK * lax.axis_size("dp"))
-    query_grad, key_grad, value_grad, owned = closing(norm_factor, layer_input[0], early, dq, dk, dv)
+    query_grad, key_grad, value_grad, owned = settled(
+        closing(norm_factor, layer_input[0], early, dq, dk, dv)
+    )
     return query_grad[None], key_grad[None], value_grad[None], owned
 
 

time: 219 us -> 212 us (0.968)
  local copies, waits for them, and re-layouts: 12.6 us -> 8.55 us
    unnamed x22 -> x18, local copies, waits for them, and re-layouts: 11.5 us -> 7.4 us
    pallas_call x1, Pallas kernels: 88.7 us -> 84.9 us  [closing(): pl.pallas_call(functools.partial(finish, norm_factor), out_shape=[jax.Sha...]
    pallas_call x0 -> x1, Pallas kernels: none -> 2.22 us  [settled(): pl.pallas_call(hand_over, out_shape=[jax.ShapeDtypeStruct(a.shape, a.dtyp...]
  transfers between devices with their start and end apart: 1 -> 1, of which waited for: 1 -> 1; matrix products, arithmetic and copies ran while one was open for 0% -> 0% of each run, Pallas kernels for 39% -> 40%
where the time goes in v4:
time: 212 us; the launch traced here: 211 us
  Pallas kernels  172 us (81%)
  waiting for transfers between devices  16.1 us (8%)
  between operations  14.2 us (7%)
  local copies, waits for them, and re-layouts  8.55 us (4%)
    pallas_call x1, Pallas kernels, closing(): pl.pallas_call(functools.partial(finish, norm_factor), out_shape=[jax.Sha...  84.9 us
    pallas_call x1, Pallas kernels, heads_exchange(): pl.pallas_call(to_heads, out_shape=[jax.ShapeDtypeStruct((tokens, COLS),...  65.7 us
    pallas_call x1, Pallas kernels, attention(): pl.pallas_call(attend, out_shape=[jax.ShapeDtypeStruct((tokens, COLS), jn...  18.8 us
    all_gather x1, waiting for transfers between devices, gather_early(): whole = lax.all_gather(mine[None], 'seq', axis=1, tiled=True)  16.1 us
    unnamed x18, local copies, waits for them, and re-layouts  7.4 us
  transfers between devices with their start and end apart: 1, of which 1 were waited for; matrix products, arithmetic and copies ran while one was open for 0% of the time, Pallas kernels for 40%

profile of v4, /device:TPU:1, one launch (start us, length us, event | category | flops | bytes accessed | tf_op | source)
XLA Modules:
  0.0 211.3 jit_solution(13573054427453129259)
XLA Ops:
  7.2 0.0 copy-start.8
  7.2 0.0 all-gather.3.cloned.1.call-start
  7.3 1.1 dynamic-slice_bitcast_fusion.1
  8.3 0.8 pad_maximum_fusion
  9.2 0.0 all-gather.3.cloned.1.call-update
  9.2 0.0 copy-done.8
  9.2 0.1 copy.11.kv_links
  9.3 0.0 copy-start.7
  9.3 65.7 %shard_map.102 = (bf16[2048,256]{1,0:T(8,128)(2,1)}, bf16[2048,256]{1,0:T(8,128)(2,1)}, bf16[2048,256]{1,0:T(8,128)(2,1)}, bf16[2048,256]{1,0:T(8,128)(2,1)}) custom-call(bf16[128,4096]{1,0:T(8,128)(2,1)} %bitcast.18, bf16[128,4096]{1,0:T(8,128)(2,1)} %bitcast.19, bf16[128,4096]{1,0:T(8,128)(2,1)} %bitcast.20, bf16[128,4096]{1,0:T(8,128)(2,1)} %bitcast.21), custom_call_target="tpu_custom_call" | custom-call | tf_op jit(solution)/shard_map/pallas_call | solution.py:77
  75.0 0.0 copy-done.7
  75.0 0.0 copy-start.3
  75.0 1.2 copy-done.3
  76.2 0.0 copy-start.4
  76.2 1.2 copy-done.4
  77.4 0.0 copy-start.5
  77.4 1.2 copy-done.5
  78.6 0.0 copy-start.6
  78.6 1.5 copy-done.6
  80.2 0.0 copy-start
  80.2 18.8 %shard_map.103 = (bf16[2048,256]{1,0:T(8,128)(2,1)S(1)}, bf16[2048,256]{1,0:T(8,128)(2,1)S(1)}, bf16[2048,256]{1,0:T(8,128)(2,1)S(1)}) custom-call(s32[16,8]{1,0:T(8,128)S(1)} %copy.11.kv_links, s32[16]{0:T(128)S(1)} %bitcast.16, bf16[2048,256]{1,0:T(8,128)(2,1)S(1)} %copy-done.3, bf16[2048,256]{1,0:T(8,128)(2,1)S(1)} %copy-done.4, ...), custom_call_target="tpu_custom_call" | custom-call | flops 5368709120 | bytes 7340032 | tf_op jit(solution)/shard_map/pallas_call | solution.py:378
  99.0 0.0 copy-start.1
  99.0 1.0 copy-done.1
  100.0 16.1 %all-gather.3.cloned.1.call-done = bf16[2048,2048]{1,0:T(8,128)(2,1)} async-done(((bf16[128,2048]{1,0:T(8,128)(2,1)}), bf16[2048,2048]{1,0:T(8,128)(2,1)}) %all-gather.3.cloned.1.call-update) | async-done | bytes 8388624 | tf_op jit(solution)/shard_map/all_gather | solution.py:404
  116.1 0.0 copy-done
  116.1 0.0 copy-start.2
  116.1 1.2 copy-done.2
  117.3 84.9 %shard_map.104 = (bf16[128,4096]{1,0:T(8,128)(2,1)S(1)}, bf16[128,4096]{1,0:T(8,128)(2,1)S(1)}, bf16[128,4096]{1,0:T(8,128)(2,1)S(1)}, f32[3,512,256]{2,1,0:T(8,128)S(1)}) custom-call(bf16[128,4096]{1,0:T(8,128)(2,1)S(1)} %bitcast.15, bf16[4,4,128,2048]{3,2,1,0:T(8,128)(2,1)} %bitcast.17, bf16[2048,256]{1,0:T(8,128)(2,1)S(1)} %get-tuple-element.23.dq_ref, ...), custom_call_target="tpu_custom_call" | custom-call | tf_op jit(solution)/shard_map/pallas_call | solution.py:272
  202.2 2.2 %shard_map.105 = (bf16[128,4096]{1,0:T(8,128)(2,1)}, bf16[128,4096]{1,0:T(8,128)(2,1)}, bf16[128,4096]{1,0:T(8,128)(2,1)}, f32[3,512,256]{2,1,0:T(8,128)}) custom-call(bf16[128,4096]{1,0:T(8,128)(2,1)S(1)} %get-tuple-element.26.refs_0_, bf16[128,4096]{1,0:T(8,128)(2,1)S(1)} %get-tuple-element.27.refs_1_, bf16[128,4096]{1,0:T(8,128)(2,1)S(1)} %get-tuple-element.28.refs_2_, ...), custom_call_target="tpu_custom_call" | custom-call | tf_op jit(solution)/shard_map/pallas_call | solution.py:418
Async XLA Ops:
  7.2 2.0 copy-start.8
  7.2 108.9 %all-gather.3.cloned.1.call-start = ((), (), s32[]{:S(2)}) async-start(), calls=%async_computation | async-start | bytes 8912896 | tf_op jit(solution)/shard_map/all_gather | solution.py:404
  9.3 65.7 %copy-start.7 = (s32[1,16]{1,0:T(1,128)S(1)}, s32[1,16]{1,0:T(1,128)}, u32[]{:S(2)}) copy-start(s32[1,16]{1,0:T(1,128)} %param.13) | copy-start | bytes 196
  75.0 1.2 copy-start.3
  76.2 1.2 copy-start.4
  77.4 1.2 copy-start.5
  78.6 1.5 copy-start.6
  80.2 35.9 %copy-start = (bf16[1,128,4096]{2,1,0:T(8,128)(2,1)S(1)}, bf16[1,128,4096]{2,1,0:T(8,128)(2,1)}, u32[]{:S(2)}) copy-start(bf16[1,128,4096]{2,1,0:T(8,128)(2,1)} %param.7) | copy-start | bytes 3145732
  99.0 1.0 copy-start.1
  116.1 1.2 copy-start.2
Sparse Core Ops, SparseCore 0:
  10.7 105.3 all-gather.2

commit v5 on v4

--- a/solution.py
+++ b/solution.py
@@ -32,6 +32,9 @@
         back = (SIDE - step) % SIDE
         place.append(lax.rem(at + step + core * (back - step), SIDE))
     return place[0] * SIDE + place[1]
+
+
+WINDOW = 1
 
 
 def block(index, size):
@@ -48,8 +51,12 @@
             barrier, inc=1, device_id={"seq": peer_of(offset)}, device_id_type=MESH
         )
     pl.semaphore_wait(barrier, SEQ - 1)
-    copies = []
+    groups = []
     for a in range(4):
+        if a >= WINDOW:
+            for copy in groups[a - WINDOW]:
+                copy.wait_send()
+        groups.append([])
         for i, offset in enumerate(OFFSETS):
             peer = peer_of(offset)
             copy = pltpu.make_async_remote_copy(
@@ -61,15 +68,22 @@
                 device_id_type=MESH,
             )
             copy.start()
-            copies.append(copy)
+            groups[a].append(copy)
+    owns = []
     for a in range(4):
         own = pltpu.make_async_copy(
             ins[a].at[:, block(me, COLS)], outs[a].at[block(me, BLK), :], own_sem.at[a]
         )
         own.start()
-        copies.append(own)
-    for copy in copies:
-        copy.wait()
+        owns.append(own)
+    for group in groups[4 - WINDOW :]:
+        for copy in group:
+            copy.wait_send()
+    for group in groups:
+        for copy in group:
+            copy.wait_recv()
+    for own in owns:
+        own.wait()
 
 
 def heads_exchange(arrays):

time: 212 us -> 206 us (0.972); the launches traced: 211 us -> 203 us
  waiting for transfers between devices: 16.1 us -> 2.02 us
  Pallas kernels: 172 us -> 178 us
    all_gather x1, waiting for transfers between devices: 16.1 us -> 2 us  [gather_early(): whole = lax.all_gather(mine[None], 'seq', axis=1, tiled=True)]
    pallas_call x1, Pallas kernels: 18.8 us -> 22.3 us  [attention(): pl.pallas_call(attend, out_shape=[jax.ShapeDtypeStruct((tokens, COLS), jn...]
  transfers between devices with their start and end apart: 1 -> 1, of which waited for: 1 -> 1; matrix products, arithmetic and copies ran while one was open for 0% -> 0% of each run, Pallas kernels for 40% -> 44%
where the time goes in v5:
time: 206 us; the launch traced here: 203 us
  Pallas kernels  178 us (86%)
  between operations  14.2 us (7%)
  local copies, waits for them, and re-layouts  8.32 us (4%)
    pallas_call x1, Pallas kernels, closing(): pl.pallas_call(functools.partial(finish, norm_factor), out_shape=[jax.Sha...  86.3 us
    pallas_call x1, Pallas kernels, heads_exchange(): pl.pallas_call(to_heads, out_shape=[jax.ShapeDtypeStruct((tokens, COLS),...  66.9 us
    pallas_call x1, Pallas kernels, attention(): pl.pallas_call(attend, out_shape=[jax.ShapeDtypeStruct((tokens, COLS), jn...  22.3 us
    unnamed x18, local copies, waits for them, and re-layouts  7.18 us
  transfers between devices with their start and end apart: 1, of which 1 were waited for; matrix products, arithmetic and copies ran while one was open for 0% of the time, Pallas kernels for 44%

profile of v5, /device:TPU:1, one launch (start us, length us, event | category | flops | bytes accessed | tf_op | source)
XLA Modules:
  0.0 203.0 jit_solution(10964055761846144160)
XLA Ops:
  7.2 0.0 copy-start.8
  7.2 0.0 all-gather.3.cloned.1.call-start
  7.3 1.1 dynamic-slice_bitcast_fusion.1
  8.3 0.8 pad_maximum_fusion
  9.2 0.0 all-gather.3.cloned.1.call-update
  9.2 0.0 copy-done.8
  9.2 0.1 copy.11.kv_links
  9.3 0.0 copy-start.7
  9.3 66.9 %shard_map.102 = (bf16[2048,256]{1,0:T(8,128)(2,1)}, bf16[2048,256]{1,0:T(8,128)(2,1)}, bf16[2048,256]{1,0:T(8,128)(2,1)}, bf16[2048,256]{1,0:T(8,128)(2,1)}) custom-call(bf16[128,4096]{1,0:T(8,128)(2,1)} %bitcast.18, bf16[128,4096]{1,0:T(8,128)(2,1)} %bitcast.19, bf16[128,4096]{1,0:T(8,128)(2,1)} %bitcast.20, bf16[128,4096]{1,0:T(8,128)(2,1)} %bitcast.21), custom_call_target="tpu_custom_call" | custom-call | tf_op jit(solution)/shard_map/pallas_call | solution.py:91
  76.2 0.0 copy-done.7
  76.2 0.0 copy-start.3
  76.2 1.3 copy-done.3
  77.5 0.0 copy-start.4
  77.5 1.2 copy-done.4
  78.7 0.0 copy-start.5
  78.7 1.3 copy-done.5
  79.9 0.0 copy-start.6
  79.9 1.2 copy-done.6
  81.2 0.0 copy-start
  81.2 22.3 %shard_map.103 = (bf16[2048,256]{1,0:T(8,128)(2,1)S(1)}, bf16[2048,256]{1,0:T(8,128)(2,1)S(1)}, bf16[2048,256]{1,0:T(8,128)(2,1)S(1)}) custom-call(s32[16,8]{1,0:T(8,128)S(1)} %copy.11.kv_links, s32[16]{0:T(128)S(1)} %bitcast.16, bf16[2048,256]{1,0:T(8,128)(2,1)S(1)} %copy-done.3, bf16[2048,256]{1,0:T(8,128)(2,1)S(1)} %copy-done.4, ...), custom_call_target="tpu_custom_call" | custom-call | flops 5368709120 | bytes 7340032 | tf_op jit(solution)/shard_map/pallas_call | solution.py:392
  103.5 0.0 copy-start.1
  103.5 1.0 copy-done.1
  104.5 2.0 all-gather.3.cloned.1.call-done
  106.5 0.0 copy-done
  106.5 0.0 copy-start.2
  106.5 1.2 copy-done.2
  107.7 86.3 %shard_map.104 = (bf16[128,4096]{1,0:T(8,128)(2,1)S(1)}, bf16[128,4096]{1,0:T(8,128)(2,1)S(1)}, bf16[128,4096]{1,0:T(8,128)(2,1)S(1)}, f32[3,512,256]{2,1,0:T(8,128)S(1)}) custom-call(bf16[128,4096]{1,0:T(8,128)(2,1)S(1)} %bitcast.15, bf16[4,4,128,2048]{3,2,1,0:T(8,128)(2,1)} %bitcast.17, bf16[2048,256]{1,0:T(8,128)(2,1)S(1)} %get-tuple-element.23.dq_ref, ...), custom_call_target="tpu_custom_call" | custom-call | tf_op jit(solution)/shard_map/pallas_call | solution.py:286
  194.0 2.2 %shard_map.105 = (bf16[128,4096]{1,0:T(8,128)(2,1)}, bf16[128,4096]{1,0:T(8,128)(2,1)}, bf16[128,4096]{1,0:T(8,128)(2,1)}, f32[3,512,256]{2,1,0:T(8,128)}) custom-call(bf16[128,4096]{1,0:T(8,128)(2,1)S(1)} %get-tuple-element.26.refs_0_, bf16[128,4096]{1,0:T(8,128)(2,1)S(1)} %get-tuple-element.27.refs_1_, bf16[128,4096]{1,0:T(8,128)(2,1)S(1)} %get-tuple-element.28.refs_2_, ...), custom_call_target="tpu_custom_call" | custom-call | tf_op jit(solution)/shard_map/pallas_call | solution.py:432
Async XLA Ops:
  7.2 2.0 copy-start.8
  7.2 99.3 %all-gather.3.cloned.1.call-start = ((), (), s32[]{:S(2)}) async-start(), calls=%async_computation | async-start | bytes 8912896 | tf_op jit(solution)/shard_map/all_gather | solution.py:418
  9.3 66.9 %copy-start.7 = (s32[1,16]{1,0:T(1,128)S(1)}, s32[1,16]{1,0:T(1,128)}, u32[]{:S(2)}) copy-start(s32[1,16]{1,0:T(1,128)} %param.13) | copy-start | bytes 196
  76.2 1.3 copy-start.3
  77.5 1.2 copy-start.4
  78.7 1.3 copy-start.5
  79.9 1.2 copy-start.6
  81.2 25.3 %copy-start = (bf16[1,128,4096]{2,1,0:T(8,128)(2,1)S(1)}, bf16[1,128,4096]{2,1,0:T(8,128)(2,1)}, u32[]{:S(2)}) copy-start(bf16[1,128,4096]{2,1,0:T(8,128)(2,1)} %param.7) | copy-start | bytes 3145732
  103.5 1.0 copy-start.1
  106.5 1.2 copy-start.2
Sparse Core Ops, SparseCore 0:
  10.7 95.7 all-gather.2

commit v6 on v5

--- a/solution.py
+++ b/solution.py
@@ -311,18 +311,27 @@
     )(layer_rows, early, dq, dk, dv)
 
 
-def attend(kv_links, tallies, q_ref, k_ref, v_ref, g_ref, dq_ref, dk_ref, dv_ref, wq, turned, acc, sp):
+def attend(kv_links, tallies, q_hbm, k_hbm, v_hbm, g_hbm, dq_ref, dk_ref, dv_ref,
+           q_ref, k_ref, v_ref, g_ref, wq, turned, acc, sp, sem):
     scale = HDIM ** (-0.5)
     heads = COLS // HDIM
     f32 = jnp.float32
+    pairs = ((k_hbm, k_ref), (q_hbm, q_ref), (v_hbm, v_ref), (g_hbm, g_ref))
+    loads = [pltpu.make_async_copy(a, b, sem.at[i]) for i, (a, b) in enumerate(pairs)]
+    for load in loads:
+        load.start()
     acc[...] = jnp.zeros_like(acc)
     wq[...] = jnp.zeros_like(wq)
+    loads[0].wait()
 
     @pl.loop(0, NQB)
     def _(n):
         rows = pl.ds(pl.multiple_of(n * BLK, BLK), BLK)
         for h in range(heads):
             turned[h, n] = k_ref[rows, h * HDIM : (h + 1) * HDIM].astype(f32).T.astype(jnp.bfloat16)
+
+    for load in loads[1:]:
+        load.wait()
 
     @pl.loop(0, NQB)
     def _(b):
@@ -392,15 +401,17 @@
     return pl.pallas_call(
         attend,
         out_shape=[jax.ShapeDtypeStruct((tokens, COLS), jnp.bfloat16)] * 3,
-        in_specs=[smem, smem] + [spec] * 4,
+        in_specs=[smem, smem] + [pl.BlockSpec(memory_space=pltpu.HBM)] * 4,
         out_specs=[spec] * 3,
-        scratch_shapes=[
+        scratch_shapes=[pltpu.VMEM((tokens, COLS), jnp.bfloat16)] * 4
+        + [
             pltpu.VMEM((heads, 2 * HDIM, 2 * BLK), jnp.bfloat16),
             pltpu.VMEM((heads, NQB, HDIM, BLK), jnp.bfloat16),
             pltpu.VMEM((heads, tokens, 2 * HDIM), jnp.float32),
             pltpu.VMEM((heads, MAXNB, BLK, 2 * BLK), jnp.float32),
+            pltpu.SemaphoreType.DMA((4,)),
         ],
-        compiler_params=pltpu.CompilerParams(vmem_limit_bytes=16 << 20),
+        compiler_params=pltpu.CompilerParams(vmem_limit_bytes=56 << 20),
         cost_estimate=pl.CostEstimate(
             flops=flops, bytes_accessed=7 * tokens * COLS * 2, transcendentals=heads * NQB * MAXNB * BLK * BLK
         ),

time: 206 us -> 207 us (level); the launches traced: 203 us -> 206 us
  waiting for transfers between devices: 2.02 us -> 7.92 us
  local copies, waits for them, and re-layouts: 8.32 us -> 5.42 us
    all_gather x1, waiting for transfers between devices: 2 us -> 7.91 us  [gather_early(): whole = lax.all_gather(mine[None], 'seq', axis=1, tiled=True)]
    unnamed x18 -> x10, local copies, waits for them, and re-layouts: 7.18 us -> 3.68 us
  transfers between devices with their start and end apart: 1 -> 1, of which waited for: 1 -> 1; matrix products, arithmetic and copies ran while one was open for 0% -> 0% of each run, Pallas kernels for 44% -> 43%
where the time goes in v6:
time: 207 us; the launch traced here: 206 us
  Pallas kernels  178 us (86%)
  between operations  14.1 us (7%)
  waiting for transfers between devices  7.92 us (4%)
  local copies, waits for them, and re-layouts  5.42 us (3%)
    pallas_call x1, Pallas kernels, closing(): pl.pallas_call(functools.partial(finish, norm_factor), out_shape=[jax.Sha...  86.6 us
    pallas_call x1, Pallas kernels, heads_exchange(): pl.pallas_call(to_heads, out_shape=[jax.ShapeDtypeStruct((tokens, COLS),...  66.9 us
    pallas_call x1, Pallas kernels, attention(): pl.pallas_call(attend, out_shape=[jax.ShapeDtypeStruct((tokens, COLS), jn...  22.1 us
    all_gather x1, waiting for transfers between devices, gather_early(): whole = lax.all_gather(mine[None], 'seq', axis=1, tiled=True)  7.91 us
  transfers between devices with their start and end apart: 1, of which 1 were waited for; matrix products, arithmetic and copies ran while one was open for 0% of the time, Pallas kernels for 43%

profile of v6, /device:TPU:1, one launch (start us, length us, event | category | flops | bytes accessed | tf_op | source)
XLA Modules:
  0.0 206.2 jit_solution(5106308477347130956)
XLA Ops:
  7.2 0.0 copy-start.4
  7.2 0.0 all-gather.3.cloned.1.call-start
  7.3 1.1 dynamic-slice_bitcast_fusion.1
  8.3 0.8 pad_maximum_fusion
  9.2 0.0 all-gather.3.cloned.1.call-update
  9.2 0.0 copy-done.4
  9.2 0.7 copy.11.kv_links
  9.9 66.9 %shard_map.102 = (bf16[2048,256]{1,0:T(8,128)(2,1)}, bf16[2048,256]{1,0:T(8,128)(2,1)}, bf16[2048,256]{1,0:T(8,128)(2,1)}, bf16[2048,256]{1,0:T(8,128)(2,1)}) custom-call(bf16[128,4096]{1,0:T(8,128)(2,1)} %bitcast.17, bf16[128,4096]{1,0:T(8,128)(2,1)} %bitcast.18, bf16[128,4096]{1,0:T(8,128)(2,1)} %bitcast.19, bf16[128,4096]{1,0:T(8,128)(2,1)} %bitcast.20), custom_call_target="tpu_custom_call" | custom-call | tf_op jit(solution)/shard_map/pallas_call | solution.py:91
  76.8 0.0 copy-start
  76.8 22.1 %shard_map.103 = (bf16[2048,256]{1,0:T(8,128)(2,1)}, bf16[2048,256]{1,0:T(8,128)(2,1)}, bf16[2048,256]{1,0:T(8,128)(2,1)}) custom-call(s32[16,8]{1,0:T(8,128)} %copy.11.kv_links, s32[16]{0:T(128)} %bitcast.25, bf16[2048,256]{1,0:T(8,128)(2,1)} %get-tuple-element.19.q_hbm, bf16[2048,256]{1,0:T(8,128)(2,1)} %get-tuple-element.20.k_hbm, ...), custom_call_target="tpu_custom_call" | custom-call | flops 5368709120 | bytes 7340032 | tf_op jit(solution)/shard_map/pallas_call | solution.py:401
  98.8 7.9 %all-gather.3.cloned.1.call-done = bf16[2048,2048]{1,0:T(8,128)(2,1)} async-done(((bf16[128,2048]{1,0:T(8,128)(2,1)}), bf16[2048,2048]{1,0:T(8,128)(2,1)}) %all-gather.3.cloned.1.call-update) | async-done | bytes 8388624 | tf_op jit(solution)/shard_map/all_gather | solution.py:429
  106.7 0.0 copy-done
  106.7 0.0 copy-start.1
  106.8 1.2 copy-done.1
  108.0 0.0 copy-start.2
  108.0 1.2 copy-done.2
  109.2 0.0 copy-start.3
  109.2 1.2 copy-done.3
  110.4 86.6 %shard_map.104 = (bf16[128,4096]{1,0:T(8,128)(2,1)S(1)}, bf16[128,4096]{1,0:T(8,128)(2,1)S(1)}, bf16[128,4096]{1,0:T(8,128)(2,1)S(1)}, f32[3,512,256]{2,1,0:T(8,128)S(1)}) custom-call(bf16[128,4096]{1,0:T(8,128)(2,1)S(1)} %bitcast.15, bf16[4,4,128,2048]{3,2,1,0:T(8,128)(2,1)} %bitcast.16, bf16[2048,256]{1,0:T(8,128)(2,1)S(1)} %copy-done.1, ...), custom_call_target="tpu_custom_call" | custom-call | tf_op jit(solution)/shard_map/pallas_call | solution.py:286
  197.1 2.2 %shard_map.105 = (bf16[128,4096]{1,0:T(8,128)(2,1)}, bf16[128,4096]{1,0:T(8,128)(2,1)}, bf16[128,4096]{1,0:T(8,128)(2,1)}, f32[3,512,256]{2,1,0:T(8,128)}) custom-call(bf16[128,4096]{1,0:T(8,128)(2,1)S(1)} %get-tuple-element.26.refs_0_, bf16[128,4096]{1,0:T(8,128)(2,1)S(1)} %get-tuple-element.27.refs_1_, bf16[128,4096]{1,0:T(8,128)(2,1)S(1)} %get-tuple-element.28.refs_2_, ...), custom_call_target="tpu_custom_call" | custom-call | tf_op jit(solution)/shard_map/pallas_call | solution.py:443
Async XLA Ops:
  7.2 2.0 copy-start.4
  7.2 99.6 %all-gather.3.cloned.1.call-start = ((), (), s32[]{:S(2)}) async-start(), calls=%async_computation | async-start | bytes 8912896 | tf_op jit(solution)/shard_map/all_gather | solution.py:429
  76.8 30.0 %copy-start = (bf16[1,128,4096]{2,1,0:T(8,128)(2,1)S(1)}, bf16[1,128,4096]{2,1,0:T(8,128)(2,1)}, u32[]{:S(2)}) copy-start(bf16[1,128,4096]{2,1,0:T(8,128)(2,1)} %param.7) | copy-start | bytes 3145732
  106.7 1.2 copy-start.1
  108.0 1.2 copy-start.2
  109.2 1.2 copy-start.3
Sparse Core Ops, SparseCore 0:
  10.7 95.9 all-gather.2
